TPU v7x, 32 devices: a whole 2x2x4 slice. The times are simulated.
32 devices in a mesh: rows: 16 (over z, y, x), heads: 2 (over core).
Axes of the slice: x: 2, y: 2, z: 4, core: 2. Of those that a mesh axis runs over, the one named last changes fastest.
Arguments:
- tokens: bfloat16 [49152, 768], P('rows'), may hold values from -6 to 6
- cotangent: bfloat16 [49152, 768], P(('rows', 'heads')), may hold values from -6 to 6
- lengths: int32 [96], P('rows'), may hold values from 1 to 512, 29491 in all
- qkv_weight: float32 [3, 768, 768], P(None, 'rows', 'heads'), may hold values from -0.3125 to 0.3125
- qkv_first: float32 [3, 768, 768], P(None, 'rows', 'heads'), may hold values from -0.0625 to 0.0625
- qkv_second: float32 [3, 768, 768], P(None, 'rows', 'heads'), may hold values from 1.4e-06 to 5.7e-06
- out_weight: float32 [768, 768], P(('rows', 'heads')), may hold values from -0.625 to 0.625
- out_first: float32 [768, 768], P(('rows', 'heads')), may hold values from -0.0625 to 0.0625
- out_second: float32 [768, 768], P(('rows', 'heads')), may hold values from 1.4e-06 to 5.7e-06
- in_weight: float32 [768, 3072], P(('rows', 'heads')), may hold values from -0.21875 to 0.21875
- in_first: float32 [768, 3072], P(('rows', 'heads')), may hold values from -0.0625 to 0.0625
- in_second: float32 [768, 3072], P(('rows', 'heads')), may hold values from 1.4e-06 to 5.7e-06
- back_weight: float32 [3072, 768], P(('rows', 'heads')), may hold values from -0.109375 to 0.109375
- back_first: float32 [3072, 768], P(('rows', 'heads')), may hold values from -0.0625 to 0.0625
- back_second: float32 [3072, 768], P(('rows', 'heads')), may hold values from 1.4e-06 to 5.7e-06
- vectors: float32 [12, 768], replicated, may hold values from -0.8 to 1.8, as said below
- vector_first: float32 [12, 768], replicated, may hold values from -0.0625 to 0.0625
- vector_second: float32 [12, 768], replicated, may hold values from 1.4e-06 to 5.7e-06
Outputs:
- block_out: float32 [49152, 768], P(('rows', 'heads'))
- grad_in: float32 [49152, 768], P(('rows', 'heads'))
- grad_norm: float32 [1], replicated
- qkv_new: float32 [3, 768, 768], P(None, 'rows', 'heads')
- qkv_first_new: float32 [3, 768, 768], P(None, 'rows', 'heads')
- qkv_second_new: float32 [3, 768, 768], P(None, 'rows', 'heads')
- out_new: float32 [768, 768], P(('rows', 'heads'))
- out_first_new: float32 [768, 768], P(('rows', 'heads'))
- out_second_new: float32 [768, 768], P(('rows', 'heads'))
- in_new: float32 [768, 3072], P(('rows', 'heads'))
- in_first_new: float32 [768, 3072], P(('rows', 'heads'))
- in_second_new: float32 [768, 3072], P(('rows', 'heads'))
- back_new: float32 [3072, 768], P(('rows', 'heads'))
- back_first_new: float32 [3072, 768], P(('rows', 'heads'))
- back_second_new: float32 [3072, 768], P(('rows', 'heads'))
- vectors_new: float32 [12, 768], replicated
- vector_first_new: float32 [12, 768], replicated
- vector_second_new: float32 [12, 768], replicated
Inputs may be any that keep to these rules, and one draw needn't show every extreme that they name: Each sequence's keys at positions lengths[i] and beyond are masked; the longest sequence has exactly 512. `vectors`: rows 3 and 6 are the norms' gains, the other rows biases.
All inputs are finite; a program needn't handle non-finite values. No bound on the sum of `lengths` on one device may be relied on, other than what follows from the above.
Results may differ from a plain program's by a relative error of at most 0.015.
The roundings to bfloat16 on the way count: a program that leaves them out, or rounds other values in their place, can miss the bound.
Values may be sent and summed in bfloat16 or wider, within the bound.
No kernel may reach another device: no remote copies, remote signals or barrier semaphores. Data moves between devices by JAX's collectives and lax.ppermute only.
A program may use at most 192 MiB of HBM per device.

v0:
```python
import jax
import jax.numpy as jnp
from jax import lax
from jax.sharding import PartitionSpec as P

HEAD_DIM = 64


eps_norm = 1e-12
clip_limit = 100.0
learn_rate = 0.08
vector_rate = 0.3
beta_one = 0.9
beta_two = 0.999
adam_eps = 1e-06
decay_rate = 0.01
step_count = 10


def layer_norm(values, gain, shift):
    center = values - jnp.mean(values, axis=-1, keepdims=True)
    spread = jnp.mean(center * center, axis=-1, keepdims=True)
    return center * lax.rsqrt(spread + eps_norm) * gain + shift


def gelu_exact(values):
    return jax.nn.gelu(values, approximate=False)


def masked_scores(queries, key_rows, length):
    scores = jnp.einsum(
        "qhe,khe->hqk", queries, key_rows, preferred_element_type=jnp.float32
    ) * HEAD_DIM ** (-0.5)
    places = lax.broadcasted_iota(jnp.int32, (1, 1, scores.shape[2]), 2)
    return jnp.where(places < length, scores, -1000000000.0)


def attend_forward(item):
    queries, key_rows, value_rows, length = item
    scores = masked_scores(queries, key_rows, length)
    highest = jnp.max(scores, axis=2, keepdims=True)
    weights = jnp.exp(scores - highest)
    total = jnp.sum(weights, axis=2, keepdims=True)
    probs = (weights / total).astype(jnp.bfloat16)
    context = jnp.einsum("hqk,khe->qhe", probs, value_rows, preferred_element_type=jnp.float32)
    return (context.astype(jnp.bfloat16), highest + jnp.log(total))


def attend_backward(item):
    queries, key_rows, value_rows, length, log_total, grad_context = item
    scores = masked_scores(queries, key_rows, length)
    probs = jnp.exp(scores - log_total)
    grad_value = jnp.einsum(
        "hqk,qhe->khe", probs.astype(jnp.bfloat16), grad_context, preferred_element_type=jnp.float32
    )
    grad_probs = jnp.einsum(
        "qhe,khe->hqk", grad_context, value_rows, preferred_element_type=jnp.float32
    )
    grad_scores = probs * (grad_probs - jnp.sum(probs * grad_probs, axis=2, keepdims=True))
    grad_scores = grad_scores.astype(jnp.bfloat16)
    scaling = HEAD_DIM ** (-0.5)
    grad_query = (
        jnp.einsum("hqk,khe->qhe", grad_scores, key_rows, preferred_element_type=jnp.float32)
        * scaling
    )
    grad_key = (
        jnp.einsum("hqk,qhe->khe", grad_scores, queries, preferred_element_type=jnp.float32)
        * scaling
    )
    return (
        grad_query.astype(jnp.bfloat16),
        grad_key.astype(jnp.bfloat16),
        grad_value.astype(jnp.bfloat16),
    )


def adam_update(weight, first, second, grad, decay, rate):
    first_new = beta_one * first + (1.0 - beta_one) * grad
    second_new = beta_two * second + (1.0 - beta_two) * grad * grad
    fix_one = 1.0 - beta_one**step_count
    fix_two = 1.0 - beta_two**step_count
    move = first_new / fix_one / (jnp.sqrt(second_new / fix_two) + adam_eps)
    return (weight - rate * (move + decay * weight), first_new, second_new)


def body(
    tokens,
    cotangent,
    lengths,
    qkv_weight,
    qkv_first,
    qkv_second,
    out_weight,
    out_first,
    out_second,
    in_weight,
    in_first,
    in_second,
    back_weight,
    back_first,
    back_second,
    vectors,
    vector_first,
    vector_second,
):
    head_index = lax.axis_index("heads")
    local = qkv_weight.shape[2]
    model = tokens.shape[1]
    tok_all = tokens.shape[0]
    tok_half = cotangent.shape[0]
    seq_count = lengths.shape[0]
    seq_len = tok_all // seq_count
    loc_heads = local // HEAD_DIM
    qkv_full = lax.all_gather(qkv_weight.astype(jnp.bfloat16), "rows", axis=1, tiled=True)
    out_full, in_full, back_full = (
        lax.all_gather(out_weight.astype(jnp.bfloat16), ("rows", "heads"), axis=0, tiled=True),
        lax.all_gather(in_weight.astype(jnp.bfloat16), ("rows", "heads"), axis=0, tiled=True),
        lax.all_gather(back_weight.astype(jnp.bfloat16), ("rows", "heads"), axis=0, tiled=True),
    )
    bias_query = lax.dynamic_slice_in_dim(vectors[0], head_index * local, local)
    bias_value = lax.dynamic_slice_in_dim(vectors[1], head_index * local, local)
    bias_inner = vectors[8:].reshape(-1)
    projected = jnp.einsum("td,jdc->jtc", tokens, qkv_full, preferred_element_type=jnp.float32)
    queries = (projected[0] + bias_query).astype(jnp.bfloat16)
    key_rows = projected[1].astype(jnp.bfloat16)
    value_rows = (projected[2] + bias_value).astype(jnp.bfloat16)

    def per_seq(array):
        return array.reshape(seq_count, seq_len, loc_heads, HEAD_DIM)

    seq_query = per_seq(queries)
    seq_key = per_seq(key_rows)
    seq_value = per_seq(value_rows)
    context, log_totals = lax.map(attend_forward, (seq_query, seq_key, seq_value, lengths))
    context = context.reshape(tok_all, local)
    ctx_tokens = lax.all_to_all(context, "heads", split_axis=0, concat_axis=1, tiled=True)
    x_half = lax.dynamic_slice_in_dim(tokens, head_index * tok_half, tok_half, 0).astype(
        jnp.float32
    )
    attn_out = jnp.dot(ctx_tokens, out_full, preferred_element_type=jnp.float32) + vectors[2]
    hidden, norm_one_pull = jax.vjp(layer_norm, x_half + attn_out, vectors[3], vectors[4])
    hidden_low = hidden.astype(jnp.bfloat16)
    inner = jnp.dot(hidden_low, in_full, preferred_element_type=jnp.float32) + bias_inner
    activ, gelu_pull = jax.vjp(gelu_exact, inner)
    activ_low = activ.astype(jnp.bfloat16)
    ffn_out = jnp.dot(activ_low, back_full, preferred_element_type=jnp.float32) + vectors[5]
    block_out, norm_two_pull = jax.vjp(layer_norm, hidden + ffn_out, vectors[6], vectors[7])
    grad_second, grad_gain_two, grad_shift_two = norm_two_pull(cotangent.astype(jnp.float32))
    grad_ffn = grad_second.astype(jnp.bfloat16)
    grad_back = jnp.dot(activ_low.T, grad_ffn, preferred_element_type=jnp.float32)
    grad_activ = jnp.dot(grad_ffn, back_full.T, preferred_element_type=jnp.float32)
    grad_inner = gelu_pull(grad_activ)[0].astype(jnp.bfloat16)
    grad_in_w = jnp.dot(hidden_low.T, grad_inner, preferred_element_type=jnp.float32)
    grad_hidden = grad_second + jnp.dot(grad_inner, in_full.T, preferred_element_type=jnp.float32)
    grad_first, grad_gain_one, grad_shift_one = norm_one_pull(grad_hidden)
    grad_attn = grad_first.astype(jnp.bfloat16)
    grad_out_w = jnp.dot(ctx_tokens.T, grad_attn, preferred_element_type=jnp.float32)
    grad_ctx = jnp.dot(grad_attn, out_full.T, preferred_element_type=jnp.float32).astype(
        jnp.bfloat16
    )
    grad_context = lax.all_to_all(grad_ctx, "heads", split_axis=1, concat_axis=0, tiled=True)
    grad_query, grad_key, grad_value = lax.map(
        attend_backward, (seq_query, seq_key, seq_value, lengths, log_totals, per_seq(grad_context))
    )
    grad_stack = jnp.stack(
        [
            grad_query.reshape(tok_all, local),
            grad_key.reshape(tok_all, local),
            grad_value.reshape(tok_all, local),
        ]
    )
    grad_qkv = jnp.einsum("td,jtc->jdc", tokens, grad_stack, preferred_element_type=jnp.float32)
    grad_tokens = jnp.einsum(
        "jtc,jdc->td", grad_stack, qkv_full, preferred_element_type=jnp.float32
    )
    grad_in = grad_first + lax.psum_scatter(
        grad_tokens.astype(jnp.bfloat16), "heads", scatter_dimension=0, tiled=True
    ).astype(jnp.float32)
    qkv_grad = lax.psum_scatter(grad_qkv, "rows", scatter_dimension=1, tiled=True)
    out_grad, in_grad, back_grad = (
        lax.psum_scatter(grad_out_w, ("rows", "heads"), scatter_dimension=0, tiled=True),
        lax.psum_scatter(grad_in_w, ("rows", "heads"), scatter_dimension=0, tiled=True),
        lax.psum_scatter(grad_back, ("rows", "heads"), scatter_dimension=0, tiled=True),
    )
    zero_row = jnp.zeros((model,), jnp.float32)
    row_query = lax.dynamic_update_slice_in_dim(
        zero_row, jnp.sum(grad_stack[0].astype(jnp.float32), axis=0), head_index * local, 0
    )
    row_value = lax.dynamic_update_slice_in_dim(
        zero_row, jnp.sum(grad_stack[2].astype(jnp.float32), axis=0), head_index * local, 0
    )
    vector_part = jnp.concatenate(
        [
            row_query[None],
            row_value[None],
            jnp.sum(grad_attn.astype(jnp.float32), axis=0)[None],
            grad_gain_one[None],
            grad_shift_one[None],
            jnp.sum(grad_ffn.astype(jnp.float32), axis=0)[None],
            grad_gain_two[None],
            grad_shift_two[None],
            jnp.sum(grad_inner.astype(jnp.float32), axis=0).reshape(-1, model),
        ],
        axis=0,
    )
    square_part = (
        jnp.sum(qkv_grad * qkv_grad)
        + jnp.sum(out_grad * out_grad)
        + jnp.sum(in_grad * in_grad)
        + jnp.sum(back_grad * back_grad)
    )
    vector_grad, square_total = lax.psum((vector_part, square_part), ("rows", "heads"))
    grad_norm = jnp.sqrt(square_total + jnp.sum(vector_grad * vector_grad))
    factor = clip_limit / jnp.maximum(grad_norm, clip_limit)
    qkv_new = adam_update(
        qkv_weight, qkv_first, qkv_second, factor * qkv_grad, decay_rate, learn_rate
    )
    out_new = adam_update(
        out_weight, out_first, out_second, factor * out_grad, decay_rate, learn_rate
    )
    in_new = adam_update(in_weight, in_first, in_second, factor * in_grad, decay_rate, learn_rate)
    back_new = adam_update(
        back_weight, back_first, back_second, factor * back_grad, decay_rate, learn_rate
    )
    vec_new = adam_update(
        vectors, vector_first, vector_second, factor * vector_grad, 0.0, vector_rate
    )
    return (
        block_out,
        grad_in,
        grad_norm.reshape(1),
        qkv_new[0],
        qkv_new[1],
        qkv_new[2],
        out_new[0],
        out_new[1],
        out_new[2],
        in_new[0],
        in_new[1],
        in_new[2],
        back_new[0],
        back_new[1],
        back_new[2],
        vec_new[0],
        vec_new[1],
        vec_new[2],
    )


def solution(mesh):
    in_specs = (
        P("rows", None),
        P(("rows", "heads"), None),
        P("rows"),
        P(None, "rows", "heads"),
        P(None, "rows", "heads"),
        P(None, "rows", "heads"),
        P(("rows", "heads"), None),
        P(("rows", "heads"), None),
        P(("rows", "heads"), None),
        P(("rows", "heads"), None),
        P(("rows", "heads"), None),
        P(("rows", "heads"), None),
        P(("rows", "heads"), None),
        P(("rows", "heads"), None),
        P(("rows", "heads"), None),
        P(),
        P(),
        P(),
    )
    out_specs = (
        P(("rows", "heads"), None),
        P(("rows", "heads"), None),
        P(),
        P(None, "rows", "heads"),
        P(None, "rows", "heads"),
        P(None, "rows", "heads"),
        P(("rows", "heads"), None),
        P(("rows", "heads"), None),
        P(("rows", "heads"), None),
        P(("rows", "heads"), None),
        P(("rows", "heads"), None),
        P(("rows", "heads"), None),
        P(("rows", "heads"), None),
        P(("rows", "heads"), None),
        P(("rows", "heads"), None),
        P(),
        P(),
        P(),
    )
    return jax.shard_map(body, mesh=mesh, in_specs=in_specs, out_specs=out_specs, check_vma=False)
```

profile of v0, /device:TPU:0, one launch (start us, length us, event | category | flops | bytes accessed | tf_op | source)
XLA Modules:
  0.0 1076.8 jit_solution(10501911551029216793)
XLA Ops:
  24.4 48.6 %all-gather.5.cloned.1.call-done = bf16[3,768,384]{2,1,0:T(8,128)(2,1)} async-done(((bf16[3,48,384]{2,1,0:T(8,128)(2,1)}), bf16[3,768,384]{2,1,0:T(8,128)(2,1)}) %all-gather.5.cloned.1.call-update) | async-done | bytes 1769488 | tf_op jit(solution)/shard_map/all_gather | solution.py:114
  73.0 8.2 convolution_bitcast_fusion
  87.3 7.4 squeeze.40
  100.0 7.4 squeeze.41
  111.3 6.0 convert_element_type.109
  123.1 55.9 %while.26 = (s32[]{:T(128)}, bf16[6,512,6,64]{1,3,2,0:T(8,128)(2,1)}, f32[6,6,512,1]{2,1,3,0:T(8,128)}, bf16[6,512,6,64]{1,3,2,0:T(8,128)(2,1)}, s32[6]{0:T(128)...) while((s32[]{:T(128)}, bf16[6,512,6,64]{1,3,2,0:T(8,128)(2,1)}, ...), condition=%wide.region_3.4_spmd, body=%wide.region_0.3_spmd.sunk | while | flops 421721600 | bytes 20554340 | solution.py:134
  184.7 6.8 all_to_all.26
  210.6 49.7 %multiply_convert_fusion.1 = (bf16[1536,3072]{1,0:T(8,128)(2,1)}, f32[1536,3072]{1,0:T(8,128)}, f32[1536,3072]{1,0:T(8,128)}) fusion(f32[3072]{0:T(1024)S(1)} %add.251, bf16[768,3072]{1,0:T(8,128)(2,1)} %all-gather.9.cloned.1.call-done, bf16[1536,768]{0,1:T(8,128)(2,1)S(1)} %fusion.86.clone.4), kind=kOutput, calls=%fused_computation.68 | convolution fusion | flops 7559184384 | bytes 54276096 | tf_op jit(solution)/shard_map/dot_general | solution.py:143
  261.1 13.6 %fusion.97 = (f32[1536]{0:T(1024)S(1)}, f32[1536,768]{0,1:T(8,128)S(1)}) fusion(f32[768]{0:T(1024)S(1)} %copy-done.36, bf16[1536,3072]{1,0:T(8,128)(2,1)} %get-tuple-element.328, bf16[3072,768]{1,0:T(8,128)(2,1)} %all-gather.11.cloned.1.call-done, f32[768]{0:T(1024)S(1)} %get-tuple-element.265, f32[768]{0:T(1024)S(1)} %get-tuple-element.266, ...), kind=kOutput, calls=%fused_computation.175 | convolution fusion | flops 7256013312 | bytes 23620608 | tf_op jit(solution)/shard_map/dot_general | solution.py:146
  285.2 26.8 %convert_reduce_fusion = (f32[3072]{0:T(1024)}, bf16[1536,3072]{1,0:T(8,128)(2,1)}) fusion(f32[1536,3072]{1,0:T(8,128)} %get-tuple-element.329, bf16[1536,768]{0,1:T(8,128)(2,1)} %get-tuple-element.321, bf16[3072,768]{1,0:T(8,128)(2,1)} %all-gather.11.cloned.1.call-done, f32[1536,3072]{1,0:T(8,128)} %get-tuple-element.343, f32[3072]{0:T(1024)S(1)} %add.251), kind=kOutput, calls=%fused_computation.66 | convolution fusion | flops 7327970304 | bytes 54288384 | tf_op jit(solution)/shard_map/dot_general | solution.py:151
  312.0 15.1 %multiply_reduce_fusion.1 = (f32[768]{0:T(1024)}, f32[1536]{0:T(1024)S(1)}, f32[768]{0:T(1024)}, f32[1536,768]{0,1:T(8,128)S(1)}) fusion(f32[1536,768]{0,1:T(8,128)S(1)} %bitcast.160, f32[1536]{0:T(1024)S(1)} %fusion.81, f32[1536]{0:T(1024)S(1)} %broadcast_multiply_fusion.1, f32[768]{0:T(1024)S(1)} %get-tuple-element.266, ...), kind=kOutput, calls=%fused_computation.100 | convolution fusion | flops 7267808256 | bytes 30726144 | tf_op jit(solution)/shard_map/dot_general | solution.py:154
  349.5 5.7 reshape.186
  361.1 104.6 %while.27 = (s32[]{:T(128)}, bf16[6,512,6,64]{1,3,2,0:T(8,128)(2,1)S(1)}, bf16[6,512,6,64]{1,3,2,0:T(8,128)(2,1)}, bf16[6,512,6,64]{1,3,2,0:T(8,128)(2,1)}, bf16...) while((s32[]{:T(128)}, ...), condition=%wide.region_14.15_spmd, body=%wide.region_12.14_spmd.sunk | while | flops 1031206400 | bytes 51211392 | solution.py:162
  465.8 6.0 copy.166
  471.7 8.7 reshape.195
  480.5 7.7 copy.167
  488.2 8.7 reshape.196
  496.9 7.7 copy.168
  504.6 8.9 reshape.197
  520.0 7.7 fusion.73
  527.7 6.3 copy.155
  534.1 10.5 bitcast_convert_fusion
  545.3 13.8 %fusion.83 = f32[768,3072]{1,0:T(8,128)} fusion(bf16[1536,3072]{1,0:T(8,128)(2,1)} %get-tuple-element.348, f32[1536,768]{0,1:T(8,128)} %copy-done.1, f32[768]{0:T(1024)S(1)} %copy-done.30, f32[768]{0:T(1024)S(1)} %get-tuple-element.266, f32[1536]{0:T(1024)S(1)} %fusion.81, f32[1536]{0:T(1024)S(1)} %broadcast_multiply_fusion.1), kind=kOutput, calls=%fused_computation.169 | convolution fusion | flops 7253655552 | bytes 23611392 | tf_op jit(solution)/shard_map/dot_general | solution.py:153
  559.2 13.4 %fusion.99 = f32[3072,768]{1,0:T(8,128)} fusion(bf16[1536,3072]{1,0:T(8,128)(2,1)} %get-tuple-element.328, bf16[1536,768]{0,1:T(8,128)(2,1)} %get-tuple-element.321), kind=kOutput, calls=%fused_computation.177 | convolution fusion | flops 7247757312 | bytes 21233664 | tf_op jit(solution)/shard_map/dot_general | solution.py:150
  577.3 6.1 copy.157
  585.0 127.8 %all-reduce.4.cloned.1.call-done = f32[3,768,384]{2,0,1:T(4,128)} async-done(((f32[3,768,384]{2,0,1:T(4,128)}), f32[3,768,384]{2,0,1:T(4,128)}) %all-reduce.4.cloned.1.call-update) | async-done | bytes 3538960
  715.8 11.0 %reduce-scatter.5.cloned.1.call-done = bf16[1536,768]{0,1:T(8,128)(2,1)} async-done(((bf16[3072,768]{0,1:T(8,128)(2,1)}), bf16[1536,768]{0,1:T(8,128)(2,1)}) %reduce-scatter.5.cloned.1.call-update) | async-done | bytes 2359312 | tf_op jit(solution)/shard_map/reduce_scatter | solution.py:176
  726.7 6.0 convert_add_fusion
  732.8 137.7 %reduce-scatter.9.cloned.1.call-done = f32[24,3072]{1,0:T(8,128)} async-done(((f32[768,3072]{1,0:T(8,128)}), f32[24,3072]{1,0:T(8,128)}) %reduce-scatter.9.cloned.1.call-update) | async-done | bytes 294928 | tf_op jit(solution)/shard_map/reduce_scatter | solution.py:182
  872.8 138.3 %reduce-scatter.11.cloned.1.call-done = f32[96,768]{1,0:T(8,128)} async-done(((f32[3072,768]{1,0:T(8,128)}), f32[96,768]{1,0:T(8,128)}) %reduce-scatter.11.cloned.1.call-update) | async-done | bytes 294928 | tf_op jit(solution)/shard_map/reduce_scatter | solution.py:183
  1013.5 6.2 copy.158
  1019.7 40.7 %all-reduce.1 = (f32[]{:T(128)}, f32[12,768]{1,0:T(8,128)}) all-reduce(f32[]{:T(128)S(6)} %add.266, f32[12,768]{1,0:T(8,128)S(1)} %concatenate.3), channel_id=1, replica_groups=mesh['rows'=16,'heads'=2] {'rows','heads'}, use_global_device_ids=true, to_apply=%region_24.25 | all-reduce | flops 9217 | bytes 73736 | tf_op jit(solution)/shard_map/psum | solution.py:212
  (286 shorter events, 286.6 us)
Async XLA Ops:
  7.2 65.8 %all-gather.5.cloned.1.call-start = ((), (), s32[]{:S(2)}) async-start(), calls=%async_computation.6 | async-start | bytes 1880064 | tf_op jit(solution)/shard_map/all_gather | solution.py:114
  8.9 191.1 %all-gather.7.cloned.1.call-start = ((), (), s32[]{:S(2)}) async-start(), calls=%async_computation.7 | async-start | bytes 1216512 | tf_op jit(solution)/shard_map/all_gather | solution.py:116
  10.4 200.1 %all-gather.9.cloned.1.call-start = ((), (), s32[]{:S(2)}) async-start(), calls=%async_computation.8 | async-start | bytes 4866048 | tf_op jit(solution)/shard_map/all_gather | solution.py:117
  12.2 248.9 %all-gather.11.cloned.1.call-start = ((), (), s32[]{:S(2)}) async-start(), calls=%async_computation.9 | async-start | bytes 4866048 | tf_op jit(solution)/shard_map/all_gather | solution.py:118
  15.6 245.5 %copy-start.29 = (f32[768]{0:T(1024)}, f32[768]{0:T(1024)S(1)}, u32[]{:S(2)}) copy-start(f32[768]{0:T(1024)S(1)} %get-tuple-element.265) | copy-start | bytes 9220
  179.0 12.5 %copy-start.3 = (bf16[6,512,6,64]{1,3,2,0:T(8,128)(2,1)}, bf16[6,512,6,64]{1,3,2,0:T(8,128)(2,1)S(1)}, u32[]{:S(2)}) copy-start(bf16[6,512,6,64]{1,3,2,0:T(8,128)(2,1)S(1)} %get-tuple-element.529) | copy-start | bytes 7077892
  194.9 8.2 all-to-all-start
  199.9 383.5 %reduce-scatter.7.cloned.1.call-start = ((), (), s32[]{:S(2)}) async-start(), calls=%async_computation.11 | async-start | bytes 2433024 | tf_op jit(solution)/shard_map/reduce_scatter | solution.py:181
  210.5 50.6 %copy-start.36 = (f32[768]{0:T(1024)S(1)}, f32[768]{0:T(1024)}, u32[]{:S(2)}) copy-start(f32[768]{0:T(1024)} %get-tuple-element.264) | copy-start | bytes 9220
  261.1 13.7 %copy-start.2 = (bf16[1536,768]{0,1:T(8,128)(2,1)S(1)}, bf16[1536,768]{0,1:T(8,128)(2,1)}, u32[]{:S(2)}) copy-start(bf16[1536,768]{0,1:T(8,128)(2,1)} %copy.140) | copy-start | bytes 7077892
  261.1 13.7 %copy-start.27 = (f32[768]{0:T(1024)S(1)}, f32[768]{0:T(1024)}, u32[]{:S(2)}) copy-start(f32[768]{0:T(1024)} %get-tuple-element.263) | copy-start | bytes 9220
  280.0 32.0 %slice-start = ((s8[4718592]{0:T(1024)(128)(4,1)}), s8[4194304]{0:T(1024)(128)(4,1)S(1)}, s32[]{:S(2)}) async-start(s8[4718592]{0:T(1024)(128)(4,1)} %bitcast.159), calls=%async_computation.15 | async-start | bytes 8388608
  285.2 26.8 %slice-start.1 = ((s8[4718592]{0:T(1024)(128)(4,1)}), s8[524288]{0:T(1024)(128)(4,1)S(1)}, s32[]{:S(2)}) async-start(s8[4718592]{0:T(1024)(128)(4,1)} %bitcast.159), calls=%async_computation.16 | async-start | bytes 1048576
  312.0 15.1 %copy-start.22 = (f32[1536]{0:T(1024)S(1)}, f32[1536]{0:T(1024)}, u32[]{:S(2)}) copy-start(f32[1536]{0:T(1024)} %copy-done.21) | copy-start | bytes 18436
  357.5 355.3 %all-reduce.4.cloned.1.call-start = ((), (), s32[]{:S(2)}) async-start(), calls=%async_computation.14 | async-start | bytes 9437184
  534.0 192.7 %reduce-scatter.5.cloned.1.call-start = ((), (), s32[]{:S(2)}) async-start(), calls=%async_computation.10 | async-start | bytes 7077888 | tf_op jit(solution)/shard_map/reduce_scatter | solution.py:176
  544.6 325.9 %reduce-scatter.9.cloned.1.call-start = ((), (), s32[]{:S(2)}) async-start(), calls=%async_computation.12 | async-start | bytes 9732096 | tf_op jit(solution)/shard_map/reduce_scatter | solution.py:182
  559.2 451.9 %reduce-scatter.11.cloned.1.call-start = ((), (), s32[]{:S(2)}) async-start(), calls=%async_computation.13 | async-start | bytes 9732096 | tf_op jit(solution)/shard_map/reduce_scatter | solution.py:183
  577.3 149.5 %copy-start.26 = (f32[1536]{0:T(1024)S(1)}, f32[1536]{0:T(1024)}, u32[]{:S(2)}) copy-start(f32[1536]{0:T(1024)} %copy-done.25) | copy-start | bytes 18436
  1013.3 51.5 %copy-start.11 = (f32[3,48,384]{2,1,0:T(8,128)S(1)}, f32[3,48,384]{2,1,0:T(8,128)}, u32[]{:S(2)}) copy-start(f32[3,48,384]{2,1,0:T(8,128)} %param.25) | copy-start | bytes 663556
  1013.3 51.5 %copy-start.19 = (f32[3,48,384]{2,1,0:T(8,128)S(1)}, f32[3,48,384]{2,1,0:T(8,128)}, u32[]{:S(2)}) copy-start(f32[3,48,384]{2,1,0:T(8,128)} %param.26) | copy-start | bytes 663556
  1013.3 51.5 %copy-start.20 = (f32[3,48,384]{2,1,0:T(8,128)S(1)}, f32[3,48,384]{2,1,0:T(8,128)}, u32[]{:S(2)}) copy-start(f32[3,48,384]{2,1,0:T(8,128)} %param.27) | copy-start | bytes 663556
  1013.4 52.4 %copy-start.7 = (f32[96,768]{1,0:T(8,128)S(1)}, f32[96,768]{1,0:T(8,128)}, u32[]{:S(2)}) copy-start(f32[96,768]{1,0:T(8,128)} %param.34) | copy-start | bytes 884740
  1013.4 52.4 %copy-start.10 = (f32[96,768]{1,0:T(8,128)S(1)}, f32[96,768]{1,0:T(8,128)}, u32[]{:S(2)}) copy-start(f32[96,768]{1,0:T(8,128)} %reduce-scatter.11.cloned.1.call-done) | copy-start | bytes 884740
  1013.4 52.4 %copy-start.13 = (f32[96,768]{1,0:T(8,128)S(1)}, f32[96,768]{1,0:T(8,128)}, u32[]{:S(2)}) copy-start(f32[96,768]{1,0:T(8,128)} %param.35) | copy-start | bytes 884740
  1013.4 52.4 %copy-start.14 = (f32[96,768]{1,0:T(8,128)S(1)}, f32[96,768]{1,0:T(8,128)}, u32[]{:S(2)}) copy-start(f32[96,768]{1,0:T(8,128)} %param.36) | copy-start | bytes 884740
  1013.4 53.5 %copy-start.8 = (f32[24,3072]{1,0:T(8,128)S(1)}, f32[24,3072]{1,0:T(8,128)}, u32[]{:S(2)}) copy-start(f32[24,3072]{1,0:T(8,128)} %param.31) | copy-start | bytes 884740
  1013.4 53.4 %copy-start.9 = (f32[24,3072]{1,0:T(8,128)S(1)}, f32[24,3072]{1,0:T(8,128)}, u32[]{:S(2)}) copy-start(f32[24,3072]{1,0:T(8,128)} %reduce-scatter.9.cloned.1.call-done) | copy-start | bytes 884740
  1013.4 53.4 %copy-start.15 = (f32[24,3072]{1,0:T(8,128)S(1)}, f32[24,3072]{1,0:T(8,128)}, u32[]{:S(2)}) copy-start(f32[24,3072]{1,0:T(8,128)} %param.32) | copy-start | bytes 884740
  1013.4 53.4 %copy-start.16 = (f32[24,3072]{1,0:T(8,128)S(1)}, f32[24,3072]{1,0:T(8,128)}, u32[]{:S(2)}) copy-start(f32[24,3072]{1,0:T(8,128)} %param.33) | copy-start | bytes 884740
  1019.7 48.3 %copy-start.17 = (f32[24,768]{1,0:T(8,128)S(1)}, f32[24,768]{1,0:T(8,128)}, u32[]{:S(2)}) copy-start(f32[24,768]{1,0:T(8,128)} %param.28) | copy-start | bytes 221188
  1019.7 48.3 %copy-start.18 = (f32[24,768]{1,0:T(8,128)S(1)}, f32[24,768]{1,0:T(8,128)}, u32[]{:S(2)}) copy-start(f32[24,768]{1,0:T(8,128)} %reduce-scatter.7.cloned.1.call-done) | copy-start | bytes 221188
  (25 other events, 103.2 us)
Sparse Core Ops, SparseCore 0:
  11.3 61.6 all-gather.4
  76.4 52.8 all-gather.6
  132.8 62.3 all-gather.8
  198.6 62.4 all-gather.10
  357.6 97.8 reduce-scatter.6
  534.1 178.5 all-reduce.3
  715.1 11.6 reduce-scatter.4
  733.6 136.7 reduce-scatter.8
  876.4 134.5 reduce-scatter.10
where the time goes:
time: 1090 us; the launch traced here: 1080 us
  waiting for transfers between devices  467 us (43%)
  matrix products  287 us (26%)
  local copies, waits for them, and re-layouts  167 us (15%)
  other arithmetic  81.6 us (7%)
  blocking collectives  46.3 us (4%)
  between operations  20.7 us (2%)
    reduce_scatter x1, waiting for transfers between devices, body(): lax.psum_scatter(grad_back, ('rows', 'heads'), scatter_dimension=0, tiled...  138 us
    reduce_scatter x1, waiting for transfers between devices, body(): lax.psum_scatter(grad_in_w, ('rows', 'heads'), scatter_dimension=0, tiled...  138 us
    unnamed x10, waiting for transfers between devices  128 us
    dot_general x1, matrix products, body(): jnp.dot(hidden_low, in_full, preferred_element_type=jnp.float32)  49.7 us
    all_gather x1, waiting for transfers between devices, body(): lax.all_gather(qkv_weight.astype(jnp.bfloat16), 'rows', axis=1, tiled=True)  48.6 us
    another operation x7, local copies, waits for them, and re-layouts, body(): jnp.stack([grad_query.reshape(tok_all, local), grad_key.reshape(tok_all,...  48.3 us
    psum x1, blocking collectives, body(): lax.psum((vector_part, square_part), ('rows', 'heads'))  40.7 us
    unnamed x99, local copies, waits for them, and re-layouts  30.7 us
  transfers between devices with their start and end apart: 10, of which 7 were waited for; matrix products, arithmetic and copies ran while one was open for 39% of the time, Pallas kernels for 0%

commit v1 on v0

v1 whole, which is shorter than its diff:
```python
import jax
import jax.numpy as jnp
from jax import lax
from jax.experimental import pallas as pl
from jax.experimental.pallas import tpu as pltpu
from jax.sharding import PartitionSpec as P

HEAD_DIM = 64
BF = jnp.bfloat16
F32 = jnp.float32
eps_norm = 1e-12


def nn(a, b):
    return jnp.dot(a, b, preferred_element_type=F32)


def nt(a, b):
    return lax.dot_general(a, b, (((1,), (1,)), ((), ())), preferred_element_type=F32)


def tn(a, b):
    return lax.dot_general(a, b, (((0,), (0,)), ((), ())), preferred_element_type=F32)


X, Y = 1, 2
Z = (0, 4, 8, 12)
PIECES = lambda first, second: tuple(
    tuple(z ^ b for z in Z) for b in (0, first, second, first ^ second))


def copy_blocks(pieces, orders, row, sem, place):
    for stream, refs in enumerate(pieces):
        masks = PIECES(*orders[stream])
        for ref, group in zip(refs, masks):
            for i, mask in enumerate(group):
                for src, dst in place(ref, stream, i, row ^ mask):
                    pltpu.make_async_copy(src, dst, sem).start()


QKV_SPLIT = (80, 64)
STREAMS = ((X, Y), (Y, X))


def qkv_place(target, cols, block):
    cut = QKV_SPLIT[0] - block

    def place(ref, stream, i, chip):
        size = QKV_SPLIT[stream]
        at = pl.multiple_of(chip * block, 16)
        piece = lambda a, b: ref.at[pl.ds(i * size + a, b - a)]
        into = lambda j, a, b: target.at[pl.ds(at + a, b - a), pl.ds(j * cols, cols)]
        if stream == 0:
            return ((piece(0, block), into(0, 0, block)), (piece(block, size), into(1, 0, cut)))
        rest = block - cut
        return ((piece(0, rest), into(1, cut, block)), (piece(rest, size), into(2, 0, block)))

    return place


def lane_mask(width, which):
    lanes = lax.broadcasted_iota(jnp.int32, (1, width), 1)
    return jnp.where(lanes // HEAD_DIM == which, 1.0, 0.0).astype(BF)


def key_rows_valid(keys, queries, length):
    return lax.broadcasted_iota(jnp.int32, (keys, queries), 0) < length


def attn_fwd_kernel(fast, info, lens, x_ref, vec_ref, *refs):
    half, seq = pl.program_id(0), pl.program_id(1)
    if fast:
        pieces, (ctx_ref, q_ref, k_ref, v_ref, lse_ref, w_ref, all_ref, sem) = refs[:16], refs[16:]
        block = all_ref.shape[1] // 16

        @pl.when((half == 0) & (seq == 0))
        def _():
            for i in range(2):
                own = pieces[8 * i:8 * i + 8]
                copy_blocks((own[:4], own[4:]), STREAMS, info[1], sem.at[i],
                            qkv_place(all_ref.at[i], ctx_ref.shape[1], block))

        for i in range(2):
            @pl.when((half == i) & (seq == 0))
            def _():
                pltpu.make_async_copy(all_ref.at[i], all_ref.at[i], sem.at[i]).wait()

        weights = all_ref[half]

        @pl.when(seq == 0)
        def _():
            w_ref[...] = weights
    else:
        w_ref, ctx_ref, q_ref, k_ref, v_ref, lse_ref = refs
        weights = w_ref[...]
    core = info[0]
    length = lens[core * pl.num_programs(1) + seq]
    cols = ctx_ref.shape[1]
    keys = x_ref.shape[0]
    start = pl.multiple_of((core ^ half) * cols, 128)
    proj = nn(x_ref[...], weights)
    q = (proj[:, :cols] + vec_ref[0:1, pl.ds(start, cols)]).astype(BF) * BF(HEAD_DIM ** -0.5)
    k = proj[:, cols:2 * cols].astype(BF)
    v = (proj[:, 2 * cols:] + vec_ref[1:2, pl.ds(start, cols)]).astype(BF)
    q_ref[...] = q
    k_ref[...] = k
    v_ref[...] = v
    valid = key_rows_valid(keys, keys, length)
    for pair in range(cols // 128):
        span = slice(128 * pair, 128 * pair + 128)
        kp, qp = k[:, span], q[:, span]
        vt = v[:, span].T
        parts = []
        for sub in range(2):
            s = nt(kp, qp * lane_mask(128, sub))
            s = jnp.where(valid, s, -1000000000.0)
            top = jnp.max(s, axis=0, keepdims=True)
            e = jnp.exp(s - top)
            total = jnp.sum(e, axis=0, keepdims=True)
            p = (e * (1.0 / total)).astype(BF)
            lse_ref[pl.ds(2 * pair + sub, 1), :] = top + jnp.log(total)
            parts.append(nn(vt[HEAD_DIM * sub:HEAD_DIM * sub + HEAD_DIM, :], p))
        ctx_ref[:, span] = jnp.concatenate(parts, axis=0).T.astype(BF)


def attn_fwd(info, lengths, tokens, wqkv, vectors, seqs, seq_len, cols):
    model = tokens.shape[1]
    tok = seqs * seq_len
    fast = len(wqkv) > 1
    weight = pl.BlockSpec((None, model, 3 * cols), lambda h, s, info, lens: (h, 0, 0))
    anywhere = pl.BlockSpec(memory_space=pl.ANY)
    grid_spec = pltpu.PrefetchScalarGridSpec(
        num_scalar_prefetch=2,
        grid=(2, seqs),
        in_specs=[
            pl.BlockSpec((seq_len, model), lambda h, s, info, lens: (info[0] * seqs + s, 0)),
            pl.BlockSpec(vectors.shape, lambda h, s, info, lens: (0, 0)),
        ] + ([anywhere] * len(wqkv) if fast else [weight]),
        out_specs=[
            pl.BlockSpec((seq_len, cols), lambda h, s, info, lens: (s, info[0] ^ h)),
            pl.BlockSpec((None, seq_len, cols), lambda h, s, info, lens: (h, s, 0)),
            pl.BlockSpec((None, seq_len, cols), lambda h, s, info, lens: (h, s, 0)),
            pl.BlockSpec((None, seq_len, cols), lambda h, s, info, lens: (h, s, 0)),
            pl.BlockSpec((None, None, 8, seq_len), lambda h, s, info, lens: (h, s, 0, 0)),
        ] + ([weight] if fast else []),
        scratch_shapes=[pltpu.VMEM((2, model, 3 * cols), BF), pltpu.SemaphoreType.DMA((2,))] if fast else [],
    )
    half_shape = jax.ShapeDtypeStruct((2, tok, cols), BF)
    return pl.pallas_call(
        lambda *refs: attn_fwd_kernel(fast, *refs),
        grid_spec=grid_spec,
        out_shape=[
            jax.ShapeDtypeStruct((tok, 2 * cols), BF),
            half_shape, half_shape, half_shape,
            jax.ShapeDtypeStruct((2, seqs, 8, seq_len), F32),
        ] + ([jax.ShapeDtypeStruct((2, model, 3 * cols), BF)] if fast else []),
        compiler_params=pltpu.CompilerParams(vmem_limit_bytes=48 << 20),
        cost_estimate=pl.CostEstimate(flops=25 * 10**9, transcendentals=tok * seq_len * 12,
                                      bytes_accessed=2 * 10 * tok * cols),
        name="attention_forward",
    )(info, lengths, tokens, vectors, *wqkv)


def attn_bwd_kernel(half, store, info, lens, x_ref, q_ref, k_ref, v_ref, dctx_ref, lse_ref,
                    dqkv_ref, bias_ref, *rest):
    seq = pl.program_id(0)
    core = info[0]
    length = lens[core * pl.num_programs(0) + seq]
    keys, cols = q_ref.shape
    valid = key_rows_valid(keys, keys, length)
    q, k, v, dc = q_ref[...], k_ref[...], v_ref[...], dctx_ref[...]
    for pair in range(cols // 128):
        span = slice(128 * pair, 128 * pair + 128)
        kp, qp, vp, dp_ = k[:, span], q[:, span], v[:, span], dc[:, span]
        kt, qt, dt = kp.T, qp.T, dp_.T
        dq, dk, dv = [], [], []
        for sub in range(2):
            rows = slice(HEAD_DIM * sub, HEAD_DIM * sub + HEAD_DIM)
            mask = lane_mask(128, sub)
            s = nt(kp, qp * mask)
            p = jnp.where(valid, jnp.exp(s - lse_ref[pl.ds(2 * pair + sub, 1), :]), 0.0)
            dv.append(nt(dt[rows, :], p.astype(BF)))
            dprob = nt(vp, dp_ * mask)
            delta = jnp.sum(p * dprob, axis=0, keepdims=True)
            ds = (p * (dprob - delta)).astype(BF)
            dk.append(nt(qt[rows, :], ds))
            dq.append(nn(kt[rows, :], ds) * HEAD_DIM ** -0.5)
        for j, val in enumerate((dq, dk, dv)):
            low = jnp.concatenate(val, axis=0).T.astype(BF)
            dqkv_ref[:, j * cols + 128 * pair:j * cols + 128 * pair + 128] = low
    low = dqkv_ref[...]

    @pl.when(seq == 0)
    def _():
        bias_ref[...] = jnp.zeros_like(bias_ref)

    bias_ref[0:1, :] += jnp.sum(low[:, :cols].astype(F32), axis=0, keepdims=True)
    bias_ref[1:2, :] += jnp.sum(low[:, 2 * cols:].astype(F32), axis=0, keepdims=True)
    if store:
        one_ref, two_ref, acc = rest
        grad = tn(x_ref[...], low)

        @pl.when(seq == 0)
        def _():
            acc[...] = grad

        @pl.when(seq > 0)
        def _():
            acc[...] += grad

        @pl.when(seq == pl.num_programs(0) - 1)
        def _():
            store(info, acc, one_ref, two_ref)


def attn_bwd(half, info, lengths, tokens, q, k, v, dctx, lse, seqs, seq_len, store=None, shapes=()):
    model = tokens.shape[1]
    cols = q.shape[2]
    tok = seqs * seq_len
    head = pl.BlockSpec((None, seq_len, cols), lambda s, info, lens: (half, s, 0))
    whole = lambda shape: pl.BlockSpec(shape, lambda s, info, lens: (0,) * len(shape))
    out_specs = [
        pl.BlockSpec((seq_len, 3 * cols), lambda s, info, lens: (s, 0)),
        whole((8, cols)),
    ]
    out_shape = [jax.ShapeDtypeStruct((tok, 3 * cols), BF), jax.ShapeDtypeStruct((8, cols), F32)]
    scratch = []
    if store:
        out_specs += [whole(s.shape) for s in shapes]
        out_shape += list(shapes)
        scratch = [pltpu.VMEM((model, 3 * cols), F32)]
    grid_spec = pltpu.PrefetchScalarGridSpec(
        num_scalar_prefetch=2,
        grid=(seqs,),
        in_specs=[
            pl.BlockSpec((seq_len, model), lambda s, info, lens: (info[0] * seqs + s, 0)),
            head, head, head,
            pl.BlockSpec((seq_len, cols), lambda s, info, lens: (s, info[0] ^ half)),
            pl.BlockSpec((None, None, 8, seq_len), lambda s, info, lens: (half, s, 0, 0)),
        ],
        out_specs=out_specs,
        scratch_shapes=scratch,
    )
    return pl.pallas_call(
        lambda *refs: attn_bwd_kernel(half, store, *refs),
        grid_spec=grid_spec,
        out_shape=out_shape,
        compiler_params=pltpu.CompilerParams(vmem_limit_bytes=48 << 20),
        cost_estimate=pl.CostEstimate(flops=25 * 10**9, transcendentals=tok * seq_len * 6,
                                      bytes_accessed=2 * 10 * tok * cols),
        name="attention_backward",
    )(info, lengths, tokens, q, k, v, dctx, lse)


TAIL_SCALE = 0.3 / 2 ** 0.5
TAIL_POLY = (0.16918733802338345, 0.17072502265423276, 0.14827808314028249, 0.215137650024653,
             -0.09509659092542666, 0.5483061894891728, -0.5127483189659462, 0.48577399370156327,
             -0.12956338680438764)


def gelu_pair(u):
    t = 1.0 / (1.0 + TAIL_SCALE * jnp.abs(u))
    bell = jnp.exp(u * u * -0.5)
    poly = jnp.full_like(u, 0.5 * TAIL_POLY[-1])
    for c in TAIL_POLY[-2::-1]:
        poly = poly * t + 0.5 * c
    tail = poly * t * bell
    cdf = jnp.where(u < 0.0, tail, 1.0 - tail)
    return u * cdf, cdf + u * (bell * (2.0 * 3.141592653589793) ** -0.5)


def norm_stats(z):
    center = z - jnp.mean(z, axis=-1, keepdims=True)
    r = lax.rsqrt(jnp.mean(center * center, axis=-1, keepdims=True) + eps_norm)
    return center * r, r


def norm_back(dy, xhat, r, gain):
    e = dy * gain
    return r * (e - jnp.mean(e, axis=-1, keepdims=True)
                - xhat * jnp.mean(e * xhat, axis=-1, keepdims=True))


def colsum(a):
    return jnp.sum(a, axis=0, keepdims=True)


def ffn_place(targets, core):
    wo, w1, w2 = targets
    model, inner = w1.shape
    block = model // 16
    wide, narrow = inner // 2, model // 2

    def place(ref, stream, i, chip):
        rows = pl.ds(i * block, block)
        if stream == 0:
            at = pl.ds(pl.multiple_of(chip * block, 16), block)
            left = pl.ds(pl.multiple_of(core * wide, 128), wide)
            right = pl.ds(pl.multiple_of(core * narrow, 128), narrow)
            return ((ref.at[rows, pl.ds(0, wide)], w1.at[at, left]),
                    (ref.at[rows, pl.ds(wide, narrow)], wo.at[at, right]))
        at = (chip * 2 + core) * (2 * block)
        return tuple((ref.at[rows, pl.ds(j * model, model)],
                      w2.at[pl.ds(pl.multiple_of(at + j * block, 16), block)]) for j in range(2))

    return place


def ffn_kernel(chunk, fast, info, x_ref, ctx_ref, cot_ref, vec_ref, b1_ref, *refs):
    step = pl.program_id(0)
    if fast:
        pieces, refs = refs[:16], refs[16:]
        both_ref, w2_ref, sem = refs[-3:]
        refs = refs[:-3]
        wide = both_ref.shape[1] - both_ref.shape[0]
        w1_ref, wo_ref = both_ref.at[:, :wide], both_ref.at[:, wide:]

        @pl.when(step == 0)
        def _():
            for i in range(2):
                half = pieces[8 * i:8 * i + 8]
                place = ffn_place((wo_ref, w1_ref, w2_ref), info[0] ^ i)
                copy_blocks((half[:4],), STREAMS[:1], info[1], sem.at[0], place)
            for i in range(2):
                half = pieces[8 * i:8 * i + 8]
                place = ffn_place((wo_ref, w1_ref, w2_ref), info[0] ^ i)
                copy_blocks(((), half[4:]), STREAMS, info[1], sem.at[1], place)
            pltpu.make_async_copy(both_ref, both_ref, sem.at[0]).wait()
            pltpu.make_async_copy(w2_ref, w2_ref, sem.at[1]).wait()
    else:
        wo_ref, w1_ref, w2_ref, *refs = refs
    (out_ref, dz1_ref, dctx_ref, h_ref, g_ref, df_ref, du_ref, da_ref, vg_ref, b1g_ref,
     slope_ref) = refs
    inner = w1_ref.shape[1]

    @pl.when(step == 0)
    def _():
        vg_ref[...] = jnp.zeros_like(vg_ref)
        b1g_ref[...] = jnp.zeros_like(b1g_ref)

    z1 = x_ref[...].astype(F32) + nn(ctx_ref[...], wo_ref[...]) + vec_ref[2:3, :]
    xhat1, r1 = norm_stats(z1)
    h = xhat1 * vec_ref[3:4, :] + vec_ref[4:5, :]
    h_low = h.astype(BF)
    h_ref[...] = h_low
    z2 = h + vec_ref[5:6, :]
    for j in range(inner // chunk):
        span = slice(j * chunk, j * chunk + chunk)
        u = nn(h_low, w1_ref[:, span]) + b1_ref[:, span]
        g, slope = gelu_pair(u)
        g = g.astype(BF)
        g_ref[:, span] = g
        slope_ref[:, span] = slope
        z2 = z2 + nn(g, w2_ref[span, :])
    xhat2, r2 = norm_stats(z2)
    out_ref[...] = xhat2 * vec_ref[6:7, :] + vec_ref[7:8, :]
    dy = cot_ref[...].astype(F32)
    vg_ref[4:5, :] += colsum(dy * xhat2)
    vg_ref[5:6, :] += colsum(dy)
    dz2 = norm_back(dy, xhat2, r2, vec_ref[6:7, :])
    df = dz2.astype(BF)
    df_ref[...] = df
    vg_ref[3:4, :] += colsum(df.astype(F32))
    dh = dz2
    for j in range(inner // chunk):
        span = slice(j * chunk, j * chunk + chunk)
        du = (nt(df, w2_ref[span, :]) * slope_ref[:, span]).astype(BF)
        du_ref[:, span] = du
        b1g_ref[:, span] += colsum(du.astype(F32))
        dh = dh + nt(du, w1_ref[:, span])
    vg_ref[1:2, :] += colsum(dh * xhat1)
    vg_ref[2:3, :] += colsum(dh)
    dz1 = norm_back(dh, xhat1, r1, vec_ref[3:4, :])
    dz1_ref[...] = dz1
    da = dz1.astype(BF)
    da_ref[...] = da
    vg_ref[0:1, :] += colsum(da.astype(F32))
    dctx_ref[...] = nt(da, wo_ref[...]).astype(BF)


def ffn(info, tokens, ctx, cotangent, weights, vectors, tile=256, chunk=768):
    tok, model = cotangent.shape
    inner = (vectors.shape[0] - 8) * model
    steps = tok // tile
    fast = len(weights) > 3
    row = pl.BlockSpec((tile, model), lambda s, info: (s, 0))
    wide = pl.BlockSpec((tile, inner), lambda s, info: (s, 0))
    whole = lambda shape: pl.BlockSpec(shape, lambda s, info: (0, 0), pipeline_mode=pl.Buffered(1))
    acc = lambda shape: pl.BlockSpec(shape, lambda s, info: (0, 0))
    grid_spec = pltpu.PrefetchScalarGridSpec(
        num_scalar_prefetch=1,
        grid=(steps,),
        in_specs=[
            pl.BlockSpec((tile, model), lambda s, info: (info[0] * steps + s, 0)),
            row, row, whole((8, model)), whole((1, inner)),
        ] + [pl.BlockSpec(memory_space=pl.ANY) if fast else whole(w.shape) for w in weights],
        out_specs=[row, row, row, row, wide, row, wide, row, acc((8, model)), acc((1, inner))],
        scratch_shapes=[pltpu.VMEM((tile, inner), F32)] + ([
            pltpu.VMEM((model, inner + model), BF), pltpu.VMEM((inner, model), BF),
            pltpu.SemaphoreType.DMA((2,))] if fast else []),
    )
    f = lambda d, dt: jax.ShapeDtypeStruct((tok, d), dt)
    return pl.pallas_call(
        lambda *refs: ffn_kernel(chunk, fast, *refs),
        grid_spec=grid_spec,
        out_shape=[f(model, F32), f(model, F32), f(model, BF), f(model, BF), f(inner, BF),
                   f(model, BF), f(inner, BF), f(model, BF),
                   jax.ShapeDtypeStruct((8, model), F32), jax.ShapeDtypeStruct((1, inner), F32)],
        compiler_params=pltpu.CompilerParams(vmem_limit_bytes=58 << 20),
        cost_estimate=pl.CostEstimate(flops=60 * 10**9, transcendentals=2 * tok * inner,
                                      bytes_accessed=tok * (4 * inner + 24 * model)),
        name="feed_forward",
    )(info, tokens, ctx, cotangent, vectors[:8], vectors[8:].reshape(1, -1), *weights)


def slot(first, second, chip, row):
    j = chip ^ row
    bit = lambda b: (j >> (b - 1)) & 1
    return bit(first) * 8 + bit(second) * 4 + (j >> 2)


def store_pair(info, order, chip, first_core, second_core, own_ref, other_ref):
    at = slot(*order, chip, info[1])
    even = info[0] == 0
    own_ref[at] = jnp.where(even, first_core, second_core).astype(BF)
    other_ref[at] = jnp.where(even, second_core, first_core).astype(BF)


def back_grad_kernel(order, info, g_ref, df_ref, own_ref, other_ref):
    step = pl.program_id(0)
    grad = tn(g_ref[...], df_ref[...])
    size = own_ref.shape[1]
    chips = grad.shape[0] // (2 * size)
    for i in range(chips):
        a, b = 2 * i * size, (2 * i + 1) * size
        store_pair(info, order, step * chips + i, grad[a:b], grad[b:b + size], own_ref, other_ref)


def back_grad(info, g, df, order, steps=4):
    tok, inner = g.shape
    model = df.shape[1]
    shape = jax.ShapeDtypeStruct((16, inner // 32, model), BF)
    full = pl.BlockSpec(shape.shape, lambda s, info: (0, 0, 0))
    return pl.pallas_call(
        lambda *refs: back_grad_kernel(order, *refs),
        grid_spec=pltpu.PrefetchScalarGridSpec(
            num_scalar_prefetch=1,
            grid=(steps,),
            in_specs=[pl.BlockSpec((tok, inner // steps), lambda s, info: (0, s)),
                      pl.BlockSpec((tok, model), lambda s, info: (0, 0))],
            out_specs=[full, full],
        ),
        out_shape=[shape, shape],
        compiler_params=pltpu.CompilerParams(vmem_limit_bytes=48 << 20),
        cost_estimate=pl.CostEstimate(flops=2 * tok * inner * model, transcendentals=0,
                                      bytes_accessed=2 * (tok * (inner + model) + inner * model)),
        name="back_grad",
    )(info, g, df)


def in_grad_kernel(order, info, h_ref, du_ref, ctx_ref, da_ref, own_ref, other_ref):
    step = pl.program_id(0)
    last = pl.num_programs(0) - 1

    def put(grad):
        size = own_ref.shape[1]
        for chip in range(16):
            a, b = 2 * chip * size, (2 * chip + 1) * size
            store_pair(info, order, chip, grad[a:b], grad[b:b + size], own_ref, other_ref)

    @pl.when(step < last)
    def _():
        put(tn(h_ref[...], du_ref[...]))

    @pl.when(step == last)
    def _():
        put(tn(ctx_ref[...], da_ref[...]))


def in_grad(info, h, du, ctx, da, order):
    tok, model = h.shape
    inner = du.shape[1]
    steps = inner // model
    shape = jax.ShapeDtypeStruct((16, model // 32, inner + model), BF)
    full = pl.BlockSpec((tok, model), lambda s, info: (0, 0))
    out = pl.BlockSpec((16, model // 32, model), lambda s, info: (0, 0, s))
    return pl.pallas_call(
        lambda *refs: in_grad_kernel(order, *refs),
        grid_spec=pltpu.PrefetchScalarGridSpec(
            num_scalar_prefetch=1,
            grid=(steps + 1,),
            in_specs=[full, pl.BlockSpec((tok, model), lambda s, info: (0, jnp.minimum(s, steps - 1))),
                      full, full],
            out_specs=[out, out],
        ),
        out_shape=[shape, shape],
        compiler_params=pltpu.CompilerParams(vmem_limit_bytes=48 << 20),
        cost_estimate=pl.CostEstimate(flops=2 * tok * model * (inner + model), transcendentals=0,
                                      bytes_accessed=2 * (tok * (inner + 3 * model) + model * (inner + model))),
        name="in_grad",
    )(info, h, du, ctx, da)


def store_qkv(info, acc, one_ref, two_ref):
    cols = one_ref.shape[2]
    block = acc.shape[0] // 16
    cut = QKV_SPLIT[0] - block
    rest = block - cut
    for chip in range(16):
        one, two = (slot(*order, chip, info[1]) for order in STREAMS)
        q, k, v = (acc[block * chip:block * chip + block, cols * j:cols * j + cols].astype(BF)
                   for j in range(3))
        one_ref[one, 0:block, :] = q
        one_ref[one, block:block + cut, :] = k[:cut]
        two_ref[two, 0:rest, :] = k[cut:]
        two_ref[two, rest:rest + block, :] = v


clip_limit = 100.0
learn_rate = 0.08
vector_rate = 0.3
beta_one = 0.9
beta_two = 0.999
adam_eps = 1e-06
decay_rate = 0.01
step_count = 10


def adam_kernel(norm_ref, *refs):
    count = len(refs) // 7
    ins, outs = refs[:4 * count], refs[4 * count:]
    norm = norm_ref[0]
    factor = clip_limit / jnp.maximum(norm, clip_limit)
    fix_one = 1.0 - beta_one**step_count
    fix_two = 1.0 - beta_two**step_count
    for i in range(count):
        weight, first, second, grad = (r[...] for r in ins[4 * i:4 * i + 4])
        decay, rate = (decay_rate, learn_rate) if i < count - 1 else (0.0, vector_rate)
        c = factor * grad
        first_new = beta_one * first + (1.0 - beta_one) * c
        second_new = beta_two * second + (1.0 - beta_two) * c * c
        move = first_new / fix_one / (jnp.sqrt(second_new / fix_two) + adam_eps)
        outs[3 * i][...] = weight - rate * (move + decay * weight)
        outs[3 * i + 1][...] = first_new
        outs[3 * i + 2][...] = second_new


def adam(norm, groups):
    flat = [a for group in groups for a in group]
    shapes = [jax.ShapeDtypeStruct(group[0].shape, F32) for group in groups for _ in range(3)]
    full = lambda a: pl.BlockSpec(a.shape, lambda i: (0,) * len(a.shape))
    return pl.pallas_call(
        adam_kernel,
        grid=(1,),
        in_specs=[pl.BlockSpec(memory_space=pltpu.SMEM)] + [full(a) for a in flat],
        out_specs=[full(s) for s in shapes],
        out_shape=shapes,
        compiler_params=pltpu.CompilerParams(vmem_limit_bytes=32 << 20),
        name="adam",
    )(norm, *flat)


def grad_in_kernel(info, dz1_ref, own_ref, other_ref, w_ref, out_ref):
    out_ref[...] = dz1_ref[...] + nt(own_ref[...], w_ref[0]) + nt(other_ref[...], w_ref[1])


def grad_input(info, dz1, own, other, wqkv, tile=512):
    tok, model = dz1.shape
    width = own.shape[1]
    row = lambda d: pl.BlockSpec((tile, d), lambda s, info: (s, 0))
    return pl.pallas_call(
        grad_in_kernel,
        grid_spec=pltpu.PrefetchScalarGridSpec(
            num_scalar_prefetch=1,
            grid=(tok // tile,),
            in_specs=[row(model), row(width), row(width),
                      pl.BlockSpec(wqkv.shape, lambda s, info: (0, 0, 0))],
            out_specs=row(model),
        ),
        out_shape=jax.ShapeDtypeStruct((tok, model), F32),
        compiler_params=pltpu.CompilerParams(vmem_limit_bytes=40 << 20),
        name="grad_input",
    )(info, dz1, own, other, wqkv)


def core_swap(a):
    return lax.ppermute(a, "heads", [(0, 1), (1, 0)])


def by_core(core, own, other, axis):
    return jnp.where(core == 0, jnp.concatenate([own, other], axis), jnp.concatenate([other, own], axis))


def gather_plain(qkv_weight, out_weight, in_weight, back_weight):
    qkv = lax.all_gather(qkv_weight.astype(BF), "rows", axis=1, tiled=True)
    own = qkv.transpose(1, 0, 2).reshape(qkv.shape[1], -1)
    wqkv = jnp.stack([own, core_swap(own)])
    wo, w1, w2 = (
        lax.all_gather(w.astype(BF), ("rows", "heads"), axis=0, tiled=True)
        for w in (out_weight, in_weight, back_weight)
    )
    return wqkv, wo, w1, w2


def rows_swap(a, mask):
    return lax.ppermute(a, "rows", [(i, i ^ mask) for i in range(16)])


def gather_stream(shard, pieces_z, order):
    first, second = order
    base = jnp.concatenate([shard, *pieces_z], axis=0)
    one = rows_swap(base, first)
    two = rows_swap(base, second)
    three = rows_swap(one, second)
    own = (base, one, two, three)
    return own, tuple(core_swap(a) for a in own)


def gather_qkv(qkv_weight):
    shard = qkv_weight.astype(BF).reshape(-1, qkv_weight.shape[2])
    zs = [rows_swap(shard, z) for z in Z[1:]]
    cut = QKV_SPLIT[0]
    (own_a, other_a), (own_b, other_b) = (
        gather_stream(part(shard), [part(z) for z in zs], order)
        for part, order in zip((lambda a: a[:cut], lambda a: a[cut:]), STREAMS))
    return (*own_a, *own_b, *other_a, *other_b)


def gather_ffn(core, out_weight, in_weight, back_weight):
    def columns(which):
        pick = lambda a: lax.dynamic_slice_in_dim(a, which * (a.shape[1] // 2), a.shape[1] // 2, 1)
        return jnp.concatenate([pick(in_weight), pick(out_weight)], axis=1).astype(BF)

    chip = by_core(core, columns(core), core_swap(columns(1 - core)), 0)
    size = chip.shape[0]
    low = back_weight.astype(BF)
    shard = jnp.concatenate([chip, low[:size], low[size:]], axis=1)
    zs = [rows_swap(shard, z) for z in Z[1:]]
    cut = chip.shape[1]
    (own_a, other_a), (own_b, other_b) = (
        gather_stream(part(shard), [part(z) for z in zs], order)
        for part, order in zip((lambda a: a[:, :cut], lambda a: a[:, cut:]), STREAMS))
    return (*own_a, *own_b, *other_a, *other_b)


def total(*terms):
    return sum(a.astype(F32) for a in terms)


def reduce_stream(own, other, order):
    first, second = order
    kept = [own, core_swap(other)]
    low = lambda a, b: total(*(t[a:b] for t in kept)).astype(BF)
    kept.append(rows_swap(low(8, 16), first))
    kept.append(rows_swap(low(4, 8), second))
    last = [rows_swap(low(i, i + 1), Z[i]) for i in range(1, 4)]
    return total(*(t[0] for t in kept), *(t[0] for t in last))


def all_sum(a):
    a = a + core_swap(a)
    for mask in (1, 2, 4, 8):
        a = a + rows_swap(a, mask)
    return a


def body(n_rows, n_cores, tokens, cotangent, lengths, qkv_weight, qkv_first, qkv_second, out_weight, out_first,
         out_second, in_weight, in_first, in_second, back_weight, back_first, back_second,
         vectors, vector_first, vector_second):
    core = lax.axis_index("heads")
    row = lax.axis_index("rows")
    info = jnp.stack([core, row]).astype(jnp.int32)
    tok, model = cotangent.shape
    seq_len = tokens.shape[0] // lengths.shape[0]
    seqs = tok // seq_len
    cols = qkv_weight.shape[2]

    if n_rows == 16 and n_cores == 2 and model % 768 == 0:
        pieces = gather_qkv(qkv_weight)
        ffn_weights = gather_ffn(core, out_weight, in_weight, back_weight)
        ctx, q, k, v, lse, wqkv = attn_fwd(info, lengths, tokens, pieces, vectors, seqs, seq_len, cols)
        out, dz1, dctx, h, g, df, du, da, vec_grad, b1_grad = ffn(
            info, tokens, ctx, cotangent, ffn_weights, vectors)
        in_order, back_order = STREAMS
        back_grad_total = reduce_stream(*back_grad(info, g, df, back_order), back_order)
        wide_grad = reduce_stream(*in_grad(info, h, du, ctx, da, in_order), in_order)
        shapes = [jax.ShapeDtypeStruct((16, rows, cols), BF) for rows in QKV_SPLIT]
        (dq_other, bias_other, *other), (dq_own, bias_own, *own) = (
            attn_bwd(i, info, lengths, tokens, q, k, v, dctx, lse, seqs, seq_len, store_qkv, shapes)
            for i in (1, 0))
        qkv_grad = jnp.concatenate(
            [reduce_stream(a, b, order) for a, b, order in zip(own, other, STREAMS)], axis=0
        ).reshape(qkv_weight.shape)
        in_grad_total = wide_grad[:, :in_weight.shape[1]]
        out_grad = wide_grad[:, in_weight.shape[1]:]
        grads = (qkv_grad, out_grad, in_grad_total, back_grad_total)
        bias = by_core(core, bias_own[:2], bias_other[:2], 1)
        vector_part = jnp.concatenate([bias, vec_grad[:6], b1_grad.reshape(-1, model)], axis=0)
        square_part = sum(jnp.sum(a * a) for a in grads)
        sums = all_sum(jnp.concatenate([vector_part, jnp.full((1, model), square_part)], axis=0))
        vector_grad, square_total = sums[:-1], sums[-1, 0]
    else:
        wqkv, wo, w1, w2 = gather_plain(qkv_weight, out_weight, in_weight, back_weight)
        ctx, q, k, v, lse = attn_fwd(
            info, lengths, tokens, (wqkv,), vectors, seqs, seq_len, cols)
        out, dz1, dctx, h, g, df, du, da, vec_grad, b1_grad = ffn(
            info, tokens, ctx, cotangent, (wo, w1, w2), vectors)
        dw2 = tn(g, df)
        dw1 = tn(h, du)
        dwo = tn(ctx, da)
        both = [attn_bwd(i, info, lengths, tokens, q, k, v, dctx, lse, seqs, seq_len) for i in (1, 0)]
        (dq_other, bias_other), (dq_own, bias_own) = both
        x_half = lax.dynamic_slice_in_dim(tokens, core * tok, tok, 0)
        dqkv = tn(x_half, dq_own) + core_swap(tn(x_half, dq_other))
        qkv_grad = lax.psum_scatter(dqkv, "rows", scatter_dimension=0, tiled=True)
        qkv_grad = qkv_grad.reshape(-1, 3, cols).transpose(1, 0, 2)
        grads = tuple(
            lax.psum_scatter(a, ("rows", "heads"), scatter_dimension=0, tiled=True)
            for a in (dwo, dw1, dw2)
        )
        bias = by_core(core, bias_own[:2], bias_other[:2], 1)
        vector_part = jnp.concatenate([bias, vec_grad[:6], b1_grad.reshape(-1, model)], axis=0)
        grads = (qkv_grad, *grads)
        square_part = sum(jnp.sum(a * a) for a in grads)
        vector_grad, square_total = lax.psum((vector_part, square_part), ("rows", "heads"))
    norm = jnp.sqrt(square_total + jnp.sum(vector_grad * vector_grad)).reshape(1)
    grad_in = grad_input(info, dz1, dq_own, dq_other, wqkv)
    new = adam(norm, [
        (qkv_weight, qkv_first, qkv_second, grads[0]),
        (out_weight, out_first, out_second, grads[1]),
        (in_weight, in_first, in_second, grads[2]),
        (back_weight, back_first, back_second, grads[3]),
        (vectors, vector_first, vector_second, vector_grad),
    ])
    return (out, grad_in, norm, *new)


def solution(mesh):
    split = P(("rows", "heads"), None)
    qkv = P(None, "rows", "heads")
    weights = (qkv,) * 3 + (split,) * 9 + (P(),) * 3
    return jax.shard_map(
        lambda *args: body(mesh.shape["rows"], mesh.shape["heads"], *args),
        mesh=mesh,
        in_specs=(P("rows", None), split, P("rows")) + weights,
        out_specs=(split, split, P()) + weights,
        check_vma=False,
    )
```

time: 1090 us -> 466 us (0.43)
  waiting for transfers between devices: 467 us -> 125 us
  matrix products: 287 us -> 0 us
  Pallas kernels: 0 us -> 191 us
  local copies, waits for them, and re-layouts: 167 us -> 32.5 us
  starting transfers between devices: 5.39 us -> 68.4 us
  other arithmetic: 81.6 us -> 33.2 us
  blocking collectives: 46.3 us -> 0 us
  between operations: 20.7 us -> 6.51 us
    dot_general x54 -> x0, matrix products: 287 us -> none  [the longest x1 49.7 us: body(): jnp.dot(hidden_low, in_full, preferred_element_type=jnp.float32)]
    reduce_scatter x4 -> x0, waiting for transfers between devices: 287 us -> none  [the longest x1 138 us: body(): lax.psum_scatter(grad_back, ('rows', 'heads'), scatter_dimension=0, tiled...]
    pallas_call x0 -> x8, Pallas kernels: none -> 191 us  [the longest x1 67.5 us: ffn(): pl.pallas_call(lambda *refs: ffn_kernel(chunk, fast, *refs), grid_spec=gr...]
    unnamed x10 -> x0, waiting for transfers between devices: 128 us -> none
    ppermute x0 -> x64, waiting for transfers between devices: none -> 125 us  [the longest x42 123 us: rows_swap(): return lax.ppermute(a, 'rows', [(i, i ^ mask) for i in range(16)])]
    ppermute x0 -> x64, starting transfers between devices: none -> 68.4 us  [the longest x42 64.5 us: rows_swap(): return lax.ppermute(a, 'rows', [(i, i ^ mask) for i in range(16)])]
    another operation x11 -> x2, local copies, waits for them, and re-layouts: 53.6 us -> 1.8 us  [the longest x7 48.3 us: body(): jnp.stack([grad_query.reshape(tok_all, local), grad_key.reshape(tok_all,...]
    all_gather x4 -> x0, waiting for transfers between devices: 49.4 us -> none  [the longest x1 48.6 us: body(): lax.all_gather(qkv_weight.astype(jnp.bfloat16), 'rows', axis=1, tiled=True)]
  transfers between devices with their start and end apart: 10 -> 64, of which waited for: 7 -> 25; matrix products, arithmetic and copies ran while one was open for 39% -> 7% of each run, Pallas kernels for 0% -> 24%
where the time goes in v1:
time: 466 us; the launch traced here: 457 us
  Pallas kernels  191 us (41%)
  waiting for transfers between devices  125 us (27%)
  starting transfers between devices  68.4 us (15%)
  other arithmetic  33.2 us (7%)
  local copies, waits for them, and re-layouts  32.5 us (7%)
  between operations  6.51 us (1%)
    ppermute x42, waiting for transfers between devices, rows_swap(): return lax.ppermute(a, 'rows', [(i, i ^ mask) for i in range(16)])  123 us
    pallas_call x1, Pallas kernels, ffn(): pl.pallas_call(lambda *refs: ffn_kernel(chunk, fast, *refs), grid_spec=gr...  67.5 us
    ppermute x42, starting transfers between devices, rows_swap(): return lax.ppermute(a, 'rows', [(i, i ^ mask) for i in range(16)])  64.5 us
    pallas_call x2, Pallas kernels, attn_bwd(): pl.pallas_call(lambda *refs: attn_bwd_kernel(half, store, *refs), grid_sp...  53 us
    pallas_call x1, Pallas kernels, attn_fwd(): pl.pallas_call(lambda *refs: attn_fwd_kernel(fast, *refs), grid_spec=grid...  32.6 us
    unnamed x100, local copies, waits for them, and re-layouts  27.5 us
    convert_element_type x12, other arithmetic, reduce_stream(): low = lambda a, b: total(*(t[a:b] for t in kept)).astype(BF)  15.8 us
    pallas_call x1, Pallas kernels, in_grad(): pl.pallas_call(lambda *refs: in_grad_kernel(order, *refs), grid_spec=pltp...  14.9 us
  transfers between devices with their start and end apart: 64, of which 25 were waited for; matrix products, arithmetic and copies ran while one was open for 7% of the time, Pallas kernels for 24%

profile of v1, /device:TPU:0, one launch (start us, length us, event | category | flops | bytes accessed | tf_op | source)
XLA Modules:
  0.0 457.3 jit_solution(13022957109519429279)
XLA Ops:
  1.6 3.1 collective-permute-start
  4.7 2.6 collective-permute-start.1
  10.5 5.5 %collective-permute-done.1 = bf16[144,384]{1,0:T(8,128)(2,1)S(1)} collective-permute-done((bf16[144,384]{1,0:T(8,128)(2,1)S(1)}, bf16[144,384]{1,0:T(8,128)(2,1)S(1)}, u32[]{:S(2)}, u32[]{:S(2)}) %collective-permute-start.1) | collective-permute-done | bytes 110624 | tf_op jit(solution)/shard_map/ppermute | solution.py:606
  23.8 7.6 %collective-permute-done.18 = bf16[48,3456]{1,0:T(8,128)(2,1)S(1)} collective-permute-done((bf16[48,3456]{1,0:T(8,128)(2,1)S(1)}, bf16[48,3456]{1,0:T(8,128)(2,1)S(1)}, u32[]{:S(2)}, u32[]{:S(2)}) %collective-permute-start.18) | collective-permute-done | bytes 331808 | tf_op jit(solution)/shard_map/ppermute | solution.py:606
  32.9 12.5 %collective-permute-done.19 = bf16[48,3456]{1,0:T(8,128)(2,1)S(1)} collective-permute-done((bf16[48,3456]{1,0:T(8,128)(2,1)S(1)}, bf16[48,3456]{1,0:T(8,128)(2,1)S(1)}, u32[]{:S(2)}, u32[]{:S(2)}) %collective-permute-start.19) | collective-permute-done | bytes 331808 | tf_op jit(solution)/shard_map/ppermute | solution.py:606
  49.1 2.5 collective-permute-done.4.refs_6_
  57.8 3.7 collective-permute-start.25
  63.9 7.4 %collective-permute-done.24.refs_11_ = bf16[192,1536]{1,0:T(8,128)(2,1)} collective-permute-done((bf16[192,1536]{1,0:T(8,128)(2,1)S(1)}, bf16[192,1536]{1,0:T(8,128)(2,1)}, u32[]{:S(2)}, u32[]{:S(2)}) %collective-permute-start.24) | collective-permute-done | bytes 589856 | tf_op jit(solution)/shard_map/ppermute | solution.py:606
  74.6 10.6 %collective-permute-done.25.refs_12_ = bf16[192,1536]{1,0:T(8,128)(2,1)S(1)} collective-permute-done((bf16[192,1536]{1,0:T(8,128)(2,1)S(1)}, bf16[192,1536]{1,0:T(8,128)(2,1)S(1)}, u32[]{:S(2)}, u32[]{:S(2)}) %collective-permute-start.25) | collective-permute-done | bytes 589856 | tf_op jit(solution)/shard_map/ppermute | solution.py:606
  89.5 11.1 %collective-permute-done.26.refs_13_ = bf16[192,1536]{1,0:T(8,128)(2,1)} collective-permute-done((bf16[192,1536]{1,0:T(8,128)(2,1)}, bf16[192,1536]{1,0:T(8,128)(2,1)}, u32[]{:S(2)}, u32[]{:S(2)}) %collective-permute-start.26) | collective-permute-done | bytes 589856 | tf_op jit(solution)/shard_map/ppermute | solution.py:606
  103.2 32.6 %attention_forward.1 = (bf16[1536,768]{1,0:T(8,128)(2,1)S(1)}, bf16[2,1536,384]{2,1,0:T(8,128)(2,1)}, bf16[2,1536,384]{2,1,0:T(8,128)(2,1)}, bf16[2,1536,384]{2,...) custom-call(s32[2]{0:T(128)S(1)} %pad_add_fusion.refs_0_.info, s32[6]{0:T(128)S(1)} %copy-done.29, ...), custom_call_target="tpu_custom_call" | custom-call | flops 24999999488 | bytes 11796480 | tf_op jit(solution)/shard_map/attention_forward/pallas_call | solution.py:149
  138.9 67.5 %feed_forward.1 = (f32[1536,768]{1,0:T(8,128)}, f32[1536,768]{1,0:T(8,128)}, bf16[1536,768]{1,0:T(8,128)(2,1)}, bf16[1536,768]{1,0:T(8,128)(2,1)}, bf16[1536,307...) custom-call(s32[2]{0:T(128)} %copy-done.25, ...), custom_call_target="tpu_custom_call" | custom-call | flops 60000002048 | bytes 47185920 | tf_op jit(solution)/shard_map/feed_forward/pallas_call | solution.py:403
  206.4 11.5 %back_grad.1 = (bf16[16,96,768]{2,1,0:T(8,128)(2,1)S(1)}, bf16[16,96,768]{2,1,0:T(8,128)(2,1)S(1)}) custom-call(s32[2]{0:T(128)S(1)} %copy-done.26, bf16[1536,3072]{1,0:T(8,128)(2,1)} %get-tuple-element.85.refs_1_, bf16[1536,768]{1,0:T(8,128)(2,1)} %get-tuple-element.86.refs_2_), custom_call_target="tpu_custom_call" | custom-call | flops 7247757312 | bytes 16515072 | tf_op jit(solution)/shard_map/back_grad/pallas_call | solution.py:444
  218.5 14.9 %in_grad.1 = (bf16[16,24,3840]{2,1,0:T(8,128)(2,1)}, bf16[16,24,3840]{2,1,0:T(8,128)(2,1)}) custom-call(s32[2]{0:T(128)S(1)} %copy-done.26, bf16[1536,768]{1,0:T(8,128)(2,1)S(1)} %copy-done.32, bf16[1536,3072]{1,0:T(8,128)(2,1)} %get-tuple-element.81.refs_2_, bf16[1536,768]{1,0:T(8,128)(2,1)S(1)} %copy-done.31, bf16[1536,768]{1,0:T(8,128)(2,1)} %get-tuple-element.82.refs_4_), custom_call_target="tpu_custom_call" | custom-call | flops 9059696640 | bytes 22413312 | tf_op jit(solution)/shard_map/in_grad/pallas_call | solution.py:487
  233.9 26.3 %attention_backward.3 = (bf16[1536,1152]{1,0:T(8,128)(2,1)}, f32[8,384]{1,0:T(8,128)S(1)}, bf16[16,80,384]{2,1,0:T(8,128)(2,1)S(1)}, bf16[16,64,384]{2,1,0:T(8,128)(2,1)S(1)}) custom-call(s32[2]{0:T(128)S(1)} %copy-done.26, s32[6]{0:T(128)S(1)} %copy-done.29, bf16[3072,768]{1,0:T(8,128)(2,1)} %refs_2_.6, bf16[2,1536,384]{2,1,0:T(8,128)(2,1)S(1)} %copy-done.33, ...), custom_call_target="tpu_custom_call" | custom-call | flops 24999999488 | bytes 11796480 | tf_op jit(solution)/shard_map/attention_backward/pallas_call | solution.py:244
  260.7 26.7 %attention_backward.2 = (bf16[1536,1152]{1,0:T(8,128)(2,1)}, f32[8,384]{1,0:T(8,128)S(1)}, bf16[16,80,384]{2,1,0:T(8,128)(2,1)S(1)}, bf16[16,64,384]{2,1,0:T(8,128)(2,1)S(1)}) custom-call(s32[2]{0:T(128)S(1)} %copy-done.26, s32[6]{0:T(128)S(1)} %copy-done.29, bf16[3072,768]{1,0:T(8,128)(2,1)} %refs_2_.6, bf16[2,1536,384]{2,1,0:T(8,128)(2,1)S(1)} %copy-done.33, ...), custom_call_target="tpu_custom_call" | custom-call | flops 24999999488 | bytes 11796480 | tf_op jit(solution)/shard_map/attention_backward/pallas_call | solution.py:244
  289.9 2.8 add_convert_fusion
  294.2 2.6 add_convert_fusion.1
  299.5 3.0 collective-permute-start.43
  309.3 28.8 %collective-permute-done.43 = bf16[4,64,384]{2,1,0:T(8,128)(2,1)S(1)} collective-permute-done((bf16[4,64,384]{2,1,0:T(8,128)(2,1)}, bf16[4,64,384]{2,1,0:T(8,128)(2,1)S(1)}, u32[]{:S(2)}, u32[]{:S(2)}) %collective-permute-start.43) | collective-permute-done | bytes 196640 | tf_op jit(solution)/shard_map/ppermute | solution.py:606
  339.1 3.3 collective-permute-start.44
  348.6 2.1 collective-permute-start.39
  360.7 5.8 %collective-permute-done.55 = bf16[4,96,768]{2,1,0:T(8,128)(2,1)S(1)} collective-permute-done((bf16[4,96,768]{2,1,0:T(8,128)(2,1)S(1)}, bf16[4,96,768]{2,1,0:T(8,128)(2,1)S(1)}, u32[]{:S(2)}, u32[]{:S(2)}) %collective-permute-start.55) | collective-permute-done | bytes 589856 | tf_op jit(solution)/shard_map/ppermute | solution.py:606
  368.0 3.0 collective-permute-start.57
  374.1 3.0 collective-permute-start.51
  381.5 2.5 multiply_reduce_fusion
  384.0 10.6 %collective-permute-done.51 = bf16[1,24,3840]{2,1,0:T(8,128)(2,1)S(1)} collective-permute-done((bf16[1,24,3840]{2,1,0:T(8,128)(2,1)S(1)}, bf16[1,24,3840]{2,1,0:T(8,128)(2,1)S(1)}, u32[]{:S(2)}, u32[]{:S(2)}) %collective-permute-start.51) | collective-permute-done | bytes 184352 | tf_op jit(solution)/shard_map/ppermute | solution.py:606
  404.4 3.6 collective-permute-done.60
  409.6 2.6 collective-permute-done.61
  412.2 2.6 collective-permute-start.62
  416.9 3.4 collective-permute-start.63
  424.3 9.8 %grad_input.1 = f32[1536,768]{1,0:T(8,128)} custom-call(s32[2]{0:T(128)S(1)} %copy-done.26, f32[1536,768]{1,0:T(8,128)} %get-tuple-element.63.dz1_ref, bf16[1536,1152]{1,0:T(8,128)(2,1)S(1)} %copy-done.2, bf16[1536,1152]{1,0:T(8,128)(2,1)S(1)} %copy-done.1, bf16[2,768,1152]{2,1,0:T(8,128)(2,1)S(1)} %copy-done), custom_call_target="tpu_custom_call" | custom-call | tf_op jit(solution)/shard_map/grad_input/pallas_call | solution.py:571
  (266 shorter events, 115.4 us)
Async XLA Ops:
  17.8 13.6 %collective-permute-start.18 = (bf16[48,3456]{1,0:T(8,128)(2,1)S(1)}, bf16[48,3456]{1,0:T(8,128)(2,1)S(1)}, u32[]{:S(2)}, u32[]{:S(2)}) collective-permute-start(bf16[48,3456]{1,0:T(8,128)(2,1)S(1)} %pad_maximum_fusion.2), channel_id=1, source_target_pairs={{0,8},{2,10},{4,12},{6,14},{8,0},{10,2},{12,4},{14,6},{16,24},{18,... | collective-permute-start | bytes 995336 | tf_op jit(solution)/shard_map/ppermute | solution.py:606
  19.5 25.9 %collective-permute-start.19 = (bf16[48,3456]{1,0:T(8,128)(2,1)S(1)}, bf16[48,3456]{1,0:T(8,128)(2,1)S(1)}, u32[]{:S(2)}, u32[]{:S(2)}) collective-permute-start(bf16[48,3456]{1,0:T(8,128)(2,1)S(1)} %pad_maximum_fusion.2), channel_id=1, source_target_pairs={{0,16},{2,18},{4,20},{6,22},{8,24},{10,26},{12,28},{14,30},{16,0},... | collective-permute-start | bytes 995336 | tf_op jit(solution)/shard_map/ppermute | solution.py:606
  20.9 25.0 %collective-permute-start.20 = (bf16[48,3456]{1,0:T(8,128)(2,1)S(1)}, bf16[48,3456]{1,0:T(8,128)(2,1)S(1)}, u32[]{:S(2)}, u32[]{:S(2)}) collective-permute-start(bf16[48,3456]{1,0:T(8,128)(2,1)S(1)} %pad_maximum_fusion.2), channel_id=1, source_target_pairs={{0,24},{2,26},{4,28},{6,30},{8,16},{10,18},{12,20},{14,22},{16,8},... | collective-permute-start | bytes 995336 | tf_op jit(solution)/shard_map/ppermute | solution.py:606
  22.2 23.8 %collective-permute-start.7 = (bf16[256,384]{1,0:T(8,128)(2,1)S(1)}, bf16[256,384]{1,0:T(8,128)(2,1)S(1)}, u32[]{:S(2)}, u32[]{:S(2)}) collective-permute-start(bf16[256,384]{1,0:T(8,128)(2,1)S(1)} %pad_maximum_fusion.5.refs_8_), channel_id=1, source_target_pairs={{0,2},{2,0},{4,6},{6,4},{8,10},{10,8},{12,14},{14,12},{16,18},{18,... | collective-permute-start | bytes 589832 | tf_op jit(solution)/shard_map/ppermute | solution.py:606
  23.7 23.9 %collective-permute-start.13 = (bf16[256,384]{1,0:T(8,128)(2,1)S(1)}, bf16[256,384]{1,0:T(8,128)(2,1)S(1)}, u32[]{:S(2)}, u32[]{:S(2)}) collective-permute-start(bf16[256,384]{1,0:T(8,128)(2,1)S(1)} %pad_maximum_fusion.5.refs_8_), channel_id=1, source_target_pairs={{0,1},{1,0},{2,3},{3,2},{4,5},{5,4},{6,7},{7,6},{8,9},{9,8},{10,11... | collective-permute-start | bytes 589832 | tf_op jit(solution)/shard_map/ppermute | solution.py:587
  31.4 17.4 %collective-permute-start.3 = (bf16[320,384]{1,0:T(8,128)(2,1)S(1)}, bf16[320,384]{1,0:T(8,128)(2,1)S(1)}, u32[]{:S(2)}, u32[]{:S(2)}) collective-permute-start(bf16[320,384]{1,0:T(8,128)(2,1)S(1)} %pad_maximum_fusion.3.refs_4_), channel_id=1, source_target_pairs={{0,2},{2,0},{4,6},{6,4},{8,10},{10,8},{12,14},{14,12},{16,18},{18,... | collective-permute-start | bytes 737288 | tf_op jit(solution)/shard_map/ppermute | solution.py:606
  53.4 19.6 %collective-permute-start.21 = (bf16[192,1920]{1,0:T(8,128)(2,1)}, bf16[192,1920]{1,0:T(8,128)(2,1)}, u32[]{:S(2)}, u32[]{:S(2)}) collective-permute-start(bf16[192,1920]{1,0:T(8,128)(2,1)} %pad_maximum_fusion.refs_6_), channel_id=1, source_target_pairs={{0,2},{2,0},{4,6},{6,4},{8,10},{10,8},{12,14},{14,12},{16,18},{18,... | collective-permute-start | bytes 2211848 | tf_op jit(solution)/shard_map/ppermute | solution.py:606
  55.0 16.3 %collective-permute-start.24 = (bf16[192,1536]{1,0:T(8,128)(2,1)S(1)}, bf16[192,1536]{1,0:T(8,128)(2,1)}, u32[]{:S(2)}, u32[]{:S(2)}) collective-permute-start(bf16[192,1536]{1,0:T(8,128)(2,1)S(1)} %pad_maximum_fusion.1.refs_10_), channel_id=1, source_target_pairs={{0,4},{2,6},{4,0},{6,2},{8,12},{10,14},{12,8},{14,10},{16,20},{18,... | collective-permute-start | bytes 1769480 | tf_op jit(solution)/shard_map/ppermute | solution.py:606
  57.8 27.3 %collective-permute-start.25 = (bf16[192,1536]{1,0:T(8,128)(2,1)S(1)}, bf16[192,1536]{1,0:T(8,128)(2,1)S(1)}, u32[]{:S(2)}, u32[]{:S(2)}) collective-permute-start(bf16[192,1536]{1,0:T(8,128)(2,1)S(1)} %pad_maximum_fusion.1.refs_10_), channel_id=1, source_target_pairs={{0,2},{2,0},{4,6},{6,4},{8,10},{10,8},{12,14},{14,12},{16,18},{18,... | collective-permute-start | bytes 1769480 | tf_op jit(solution)/shard_map/ppermute | solution.py:606
  61.5 25.2 %collective-permute-start.31 = (bf16[192,1536]{1,0:T(8,128)(2,1)S(1)}, bf16[192,1536]{1,0:T(8,128)(2,1)S(1)}, u32[]{:S(2)}, u32[]{:S(2)}) collective-permute-start(bf16[192,1536]{1,0:T(8,128)(2,1)S(1)} %pad_maximum_fusion.1.refs_10_), channel_id=1, source_target_pairs={{0,1},{1,0},{2,3},{3,2},{4,5},{5,4},{6,7},{7,6},{8,9},{9,8},{10,11... | collective-permute-start | bytes 1769480 | tf_op jit(solution)/shard_map/ppermute | solution.py:587
  63.9 24.9 %collective-permute-start.22 = (bf16[192,1920]{1,0:T(8,128)(2,1)}, bf16[192,1920]{1,0:T(8,128)(2,1)}, u32[]{:S(2)}, u32[]{:S(2)}) collective-permute-start(bf16[192,1920]{1,0:T(8,128)(2,1)} %pad_maximum_fusion.refs_6_), channel_id=1, source_target_pairs={{0,4},{2,6},{4,0},{6,2},{8,12},{10,14},{12,8},{14,10},{16,20},{18,... | collective-permute-start | bytes 2211848 | tf_op jit(solution)/shard_map/ppermute | solution.py:606
  71.3 18.0 %collective-permute-start.27 = (bf16[192,1920]{1,0:T(8,128)(2,1)}, bf16[192,1920]{1,0:T(8,128)(2,1)}, u32[]{:S(2)}, u32[]{:S(2)}) collective-permute-start(bf16[192,1920]{1,0:T(8,128)(2,1)} %pad_maximum_fusion.refs_6_), channel_id=1, source_target_pairs={{0,1},{1,0},{2,3},{3,2},{4,5},{5,4},{6,7},{7,6},{8,9},{9,8},{10,11... | collective-permute-start | bytes 2211848 | tf_op jit(solution)/shard_map/ppermute | solution.py:587
  73.0 29.2 %collective-permute-start.23 = (bf16[192,1920]{1,0:T(8,128)(2,1)}, bf16[192,1920]{1,0:T(8,128)(2,1)}, u32[]{:S(2)}, u32[]{:S(2)}) collective-permute-start(bf16[192,1920]{1,0:T(8,128)(2,1)} %collective-permute-done.21.refs_7_), channel_id=1, source_target_pairs={{0,4},{2,6},{4,0},{6,2},{8,12},{10,14},{12,8},{14,10},{16,20},{18,... | collective-permute-start | bytes 2211848 | tf_op jit(solution)/shard_map/ppermute | solution.py:606
  85.1 15.4 %collective-permute-start.26 = (bf16[192,1536]{1,0:T(8,128)(2,1)}, bf16[192,1536]{1,0:T(8,128)(2,1)}, u32[]{:S(2)}, u32[]{:S(2)}) collective-permute-start(bf16[192,1536]{1,0:T(8,128)(2,1)} %collective-permute-done.24.refs_11_), channel_id=1, source_target_pairs={{0,2},{2,0},{4,6},{6,4},{8,10},{10,8},{12,14},{14,12},{16,18},{18,... | collective-permute-start | bytes 1769480 | tf_op jit(solution)/shard_map/ppermute | solution.py:606
  88.8 48.3 %collective-permute-start.33 = (bf16[192,1536]{1,0:T(8,128)(2,1)}, bf16[192,1536]{1,0:T(8,128)(2,1)S(1)}, u32[]{:S(2)}, u32[]{:S(2)}) collective-permute-start(bf16[192,1536]{1,0:T(8,128)(2,1)} %copy-done.45), channel_id=1, source_target_pairs={{0,1},{1,0},{2,3},{3,2},{4,5},{5,4},{6,7},{7,6},{8,9},{9,8},{10,11... | collective-permute-start | bytes 1769480 | tf_op jit(solution)/shard_map/ppermute | solution.py:587
  89.4 47.8 %collective-permute-start.28 = (bf16[192,1920]{1,0:T(8,128)(2,1)}, bf16[192,1920]{1,0:T(8,128)(2,1)S(1)}, u32[]{:S(2)}, u32[]{:S(2)}) collective-permute-start(bf16[192,1920]{1,0:T(8,128)(2,1)} %collective-permute-done.21.refs_7_), channel_id=1, source_target_pairs={{0,1},{1,0},{2,3},{3,2},{4,5},{5,4},{6,7},{7,6},{8,9},{9,8},{10,11... | collective-permute-start | bytes 2211848 | tf_op jit(solution)/shard_map/ppermute | solution.py:587
  100.5 36.7 %collective-permute-start.29 = (bf16[192,1920]{1,0:T(8,128)(2,1)}, bf16[192,1920]{1,0:T(8,128)(2,1)S(1)}, u32[]{:S(2)}, u32[]{:S(2)}) collective-permute-start(bf16[192,1920]{1,0:T(8,128)(2,1)} %collective-permute-done.22.refs_8_), channel_id=1, source_target_pairs={{0,1},{1,0},{2,3},{3,2},{4,5},{5,4},{6,7},{7,6},{8,9},{9,8},{10,11... | collective-permute-start | bytes 2211848 | tf_op jit(solution)/shard_map/ppermute | solution.py:587
  100.5 36.7 %collective-permute-start.34 = (bf16[192,1536]{1,0:T(8,128)(2,1)}, bf16[192,1536]{1,0:T(8,128)(2,1)S(1)}, u32[]{:S(2)}, u32[]{:S(2)}) collective-permute-start(bf16[192,1536]{1,0:T(8,128)(2,1)} %collective-permute-done.26.refs_13_), channel_id=1, source_target_pairs={{0,1},{1,0},{2,3},{3,2},{4,5},{5,4},{6,7},{7,6},{8,9},{9,8},{10,11... | collective-permute-start | bytes 1769480 | tf_op jit(solution)/shard_map/ppermute | solution.py:587
  102.2 35.0 %collective-permute-start.30 = (bf16[192,1920]{1,0:T(8,128)(2,1)}, bf16[192,1920]{1,0:T(8,128)(2,1)S(1)}, u32[]{:S(2)}, u32[]{:S(2)}) collective-permute-start(bf16[192,1920]{1,0:T(8,128)(2,1)} %collective-permute-done.23.refs_9_), channel_id=1, source_target_pairs={{0,1},{1,0},{2,3},{3,2},{4,5},{5,4},{6,7},{7,6},{8,9},{9,8},{10,11... | collective-permute-start | bytes 2211848 | tf_op jit(solution)/shard_map/ppermute | solution.py:587
  217.9 76.3 %collective-permute-start.53 = (bf16[16,96,768]{2,1,0:T(8,128)(2,1)S(1)}, bf16[16,96,768]{2,1,0:T(8,128)(2,1)}, u32[]{:S(2)}, u32[]{:S(2)}) collective-permute-start(bf16[16,96,768]{2,1,0:T(8,128)(2,1)S(1)} %get-tuple-element.88), channel_id=1, source_target_pairs={{0,1},{1,0},{2,3},{3,2},{4,5},{5,4},{6,7},{7,6},{8,9},{9,8},{10,11... | collective-permute-start | bytes 7077896 | tf_op jit(solution)/shard_map/ppermute | solution.py:587
  233.3 56.6 %collective-permute-start.47 = (bf16[16,24,3840]{2,1,0:T(8,128)(2,1)}, bf16[16,24,3840]{2,1,0:T(8,128)(2,1)}, u32[]{:S(2)}, u32[]{:S(2)}) collective-permute-start(bf16[16,24,3840]{2,1,0:T(8,128)(2,1)} %get-tuple-element.84), channel_id=1, source_target_pairs={{0,1},{1,0},{2,3},{3,2},{4,5},{5,4},{6,7},{7,6},{8,9},{9,8},{10,11... | collective-permute-start | bytes 8847368 | tf_op jit(solution)/shard_map/ppermute | solution.py:587
  260.2 29.0 %collective-permute-start.35 = (bf16[16,80,384]{2,1,0:T(8,128)(2,1)S(1)}, bf16[16,80,384]{2,1,0:T(8,128)(2,1)S(1)}, u32[]{:S(2)}, u32[]{:S(2)}) collective-permute-start(bf16[16,80,384]{2,1,0:T(8,128)(2,1)S(1)} %get-tuple-element.77), channel_id=1, source_target_pairs={{0,1},{1,0},{2,3},{3,2},{4,5},{5,4},{6,7},{7,6},{8,9},{9,8},{10,11... | collective-permute-start | bytes 2949128 | tf_op jit(solution)/shard_map/ppermute | solution.py:587
  260.2 27.3 %collective-permute-start.41 = (bf16[16,64,384]{2,1,0:T(8,128)(2,1)S(1)}, bf16[16,64,384]{2,1,0:T(8,128)(2,1)S(1)}, u32[]{:S(2)}, u32[]{:S(2)}) collective-permute-start(bf16[16,64,384]{2,1,0:T(8,128)(2,1)S(1)} %get-tuple-element.79), channel_id=1, source_target_pairs={{0,1},{1,0},{2,3},{3,2},{4,5},{5,4},{6,7},{7,6},{8,9},{9,8},{10,11... | collective-permute-start | bytes 2359304 | tf_op jit(solution)/shard_map/ppermute | solution.py:587
  289.3 14.2 %collective-permute-start.36 = (bf16[8,80,384]{2,1,0:T(8,128)(2,1)S(1)}, bf16[8,80,384]{2,1,0:T(8,128)(2,1)S(1)}, u32[]{:S(2)}, u32[]{:S(2)}) collective-permute-start(bf16[8,80,384]{2,1,0:T(8,128)(2,1)S(1)} %add_convert_fusion.4), channel_id=1, source_target_pairs={{0,2},{2,0},{4,6},{6,4},{8,10},{10,8},{12,14},{14,12},{16,18},{18,... | collective-permute-start | bytes 1474568 | tf_op jit(solution)/shard_map/ppermute | solution.py:606
  292.8 55.8 %collective-permute-start.48 = (bf16[8,24,3840]{2,1,0:T(8,128)(2,1)}, bf16[8,24,3840]{2,1,0:T(8,128)(2,1)}, u32[]{:S(2)}, u32[]{:S(2)}) collective-permute-start(bf16[8,24,3840]{2,1,0:T(8,128)(2,1)} %add_convert_fusion), channel_id=1, source_target_pairs={{0,2},{2,0},{4,6},{6,4},{8,10},{10,8},{12,14},{14,12},{16,18},{18,... | collective-permute-start | bytes 4423688 | tf_op jit(solution)/shard_map/ppermute | solution.py:606
  296.9 49.2 %collective-permute-start.54 = (bf16[8,96,768]{2,1,0:T(8,128)(2,1)}, bf16[8,96,768]{2,1,0:T(8,128)(2,1)}, u32[]{:S(2)}, u32[]{:S(2)}) collective-permute-start(bf16[8,96,768]{2,1,0:T(8,128)(2,1)} %add_convert_fusion.1), channel_id=1, source_target_pairs={{0,4},{2,6},{4,0},{6,2},{8,12},{10,14},{12,8},{14,10},{16,20},{18,... | collective-permute-start | bytes 3538952 | tf_op jit(solution)/shard_map/ppermute | solution.py:606
  299.5 38.6 %collective-permute-start.43 = (bf16[4,64,384]{2,1,0:T(8,128)(2,1)}, bf16[4,64,384]{2,1,0:T(8,128)(2,1)S(1)}, u32[]{:S(2)}, u32[]{:S(2)}) collective-permute-start(bf16[4,64,384]{2,1,0:T(8,128)(2,1)} %add_convert_fusion.7), channel_id=1, source_target_pairs={{0,2},{2,0},{4,6},{6,4},{8,10},{10,8},{12,14},{14,12},{16,18},{18,... | collective-permute-start | bytes 589832 | tf_op jit(solution)/shard_map/ppermute | solution.py:606
  304.3 39.2 %collective-permute-start.37 = (bf16[4,80,384]{2,1,0:T(8,128)(2,1)}, bf16[4,80,384]{2,1,0:T(8,128)(2,1)}, u32[]{:S(2)}, u32[]{:S(2)}) collective-permute-start(bf16[4,80,384]{2,1,0:T(8,128)(2,1)} %add_convert_fusion.6), channel_id=1, source_target_pairs={{0,4},{2,6},{4,0},{6,2},{8,12},{10,14},{12,8},{14,10},{16,20},{18,... | collective-permute-start | bytes 737288 | tf_op jit(solution)/shard_map/ppermute | solution.py:606
  354.3 18.1 %collective-permute-start.49 = (bf16[4,24,3840]{2,1,0:T(8,128)(2,1)S(1)}, bf16[4,24,3840]{2,1,0:T(8,128)(2,1)S(1)}, u32[]{:S(2)}, u32[]{:S(2)}) collective-permute-start(bf16[4,24,3840]{2,1,0:T(8,128)(2,1)S(1)} %add_convert_fusion.2), channel_id=1, source_target_pairs={{0,4},{2,6},{4,0},{6,2},{8,12},{10,14},{12,8},{14,10},{16,20},{18,... | collective-permute-start | bytes 2211848 | tf_op jit(solution)/shard_map/ppermute | solution.py:606
  374.1 20.5 %collective-permute-start.51 = (bf16[1,24,3840]{2,1,0:T(8,128)(2,1)S(1)}, bf16[1,24,3840]{2,1,0:T(8,128)(2,1)S(1)}, u32[]{:S(2)}, u32[]{:S(2)}) collective-permute-start(bf16[1,24,3840]{2,1,0:T(8,128)(2,1)S(1)} %get-tuple-element.108), channel_id=1, source_target_pairs={{0,16},{2,18},{4,20},{6,22},{8,24},{10,26},{12,28},{14,30},{16,0},... | collective-permute-start | bytes 552968 | tf_op jit(solution)/shard_map/ppermute | solution.py:606
  378.0 16.6 %collective-permute-start.52 = (bf16[1,24,3840]{2,1,0:T(8,128)(2,1)S(1)}, bf16[1,24,3840]{2,1,0:T(8,128)(2,1)S(1)}, u32[]{:S(2)}, u32[]{:S(2)}) collective-permute-start(bf16[1,24,3840]{2,1,0:T(8,128)(2,1)S(1)} %get-tuple-element.107), channel_id=1, source_target_pairs={{0,24},{2,26},{4,28},{6,30},{8,16},{10,18},{12,20},{14,22},{16,8},... | collective-permute-start | bytes 552968 | tf_op jit(solution)/shard_map/ppermute | solution.py:606
  416.9 17.2 %collective-permute-start.63 = (f32[13,768]{1,0:T(8,128)S(1)}, f32[13,768]{1,0:T(8,128)S(1)}, u32[]{:S(2)}, u32[]{:S(2)}) collective-permute-start(f32[13,768]{1,0:T(8,128)S(1)} %add.361), channel_id=1, source_target_pairs={{0,16},{2,18},{4,20},{6,22},{8,24},{10,26},{12,28},{14,30},{16,0},... | collective-permute-start | bytes 119816 | tf_op jit(solution)/shard_map/ppermute | solution.py:606
  (81 other events, 923.0 us)
